TPU v7x, 128 devices: a whole 4x4x4 slice. The times are simulated.
128 devices in a mesh: dp: 32 (over z, y, core), tensor: 4 (over x).
Axes of the slice: x: 4, y: 4, z: 4, core: 2. Of those that a mesh axis runs over, the one named last changes fastest.
Arguments:
- block_input: bfloat16 [12288, 2560], P('dp', 'tensor'), may hold values from -6 to 6
- gate_act: bfloat16 [12288, 6912], P('dp', 'tensor'), may hold values from -8 to 8
- grad_out: bfloat16 [12288, 2560], P('dp', 'tensor'), may hold values from -8 to 8
- up_weight: bfloat16 [2560, 6912], P('dp', 'tensor'), may hold values from -0.125 to 0.125
- down_weight: bfloat16 [6912, 2560], P('tensor', 'dp'), may hold values from -0.078125 to 0.078125
- quant_step: float32 [6912], P('tensor'), as said below
- round_logit: float32 [2560, 6912], P('dp', 'tensor'), may hold values from -48 to 48
- grid_offset: bfloat16 [2560, 6912], P('dp', 'tensor'), may hold values from 0 to 1
Outputs:
- block_output: bfloat16 [12288, 2560], P('dp', 'tensor')
- fisher: bfloat16 [12288, 6912], P('dp', 'tensor')
- grad_logit: float32 [2560, 6912], P('dp', 'tensor')
- loss: float32 [], replicated
Inputs may be any that keep to these rules, and one draw needn't show every extreme that they name: `quant_step`: positive steps between 0.8 and 3.2 divided by the square root of 2560.
All inputs are finite; a program needn't handle non-finite values.
Results may differ from a plain program's by a relative error of at most 0.022.
Values may be sent and summed in bfloat16 or wider, within the bound.
A program may use at most 128 MiB of HBM per device.

v0:
```python
import functools

import jax
import jax.numpy as jnp
from jax import lax
from jax.sharding import Mesh
from jax.sharding import PartitionSpec as P

D = 2560
FFW = 6912
DP = ("dp_0", "dp_1", "dp_2")
DP_TENSOR = ("dp_0", "dp_1", "dp_2", "tensor")


reg_weight = 0.5


def side_by_side(arrays, axis, dim, along):
    both = jnp.concatenate(arrays, axis=along)
    whole, at, outs = (lax.all_gather(both, axis, axis=dim, tiled=True), 0, [])
    for a in arrays:
        outs.append(lax.slice_in_dim(whole, at, at + a.shape[along], axis=along))
        at += a.shape[along]
    return tuple(outs)


def in_blocks(array, dim, count):
    before, after = (array.shape[:dim], array.shape[dim + 1 :])
    return jnp.moveaxis(array.reshape(*before, count, -1, *after), dim, 0)


def sum_at_owner(array, axis, dim):
    count = lax.axis_size(axis)
    tiles = lax.all_to_all(in_blocks(array, dim, count), axis, 0, 0, tiled=True)
    return jnp.sum(tiles.astype(jnp.float32), axis=0)


def by_axis(array, axes):
    return functools.reduce(lax.psum, axes, array)


def body(
    block_input, gate_act, grad_out, up_weight, down_weight, quant_step, round_logit, grid_offset
):
    features, out_grads = side_by_side((block_input, grad_out), "tensor", 1, 0)
    tok_rows = features.shape[0]
    ff_cols = gate_act.shape[1]
    gate_vals = gate_act.astype(jnp.float32)
    soft_bits = jax.nn.sigmoid(round_logit)
    weight_delta = (quant_step[None, :] * (soft_bits - grid_offset.astype(jnp.float32))).astype(
        jnp.bfloat16
    )
    up_full, delta_full = side_by_side((up_weight, weight_delta), DP, 0, 1)
    up_proj = jnp.dot(features, up_full, preferred_element_type=jnp.float32)
    hidden = (gate_vals * up_proj).astype(jnp.bfloat16)
    down_full = lax.all_gather(down_weight, DP, axis=1, tiled=True)
    partial_out = jnp.dot(hidden, down_full, preferred_element_type=jnp.float32)
    grad_hidden = lax.dot_general(
        out_grads, down_full, (((1,), (1,)), ((), ())), preferred_element_type=jnp.float32
    )
    residual = jnp.dot(features, delta_full, preferred_element_type=jnp.float32)
    block_output = sum_at_owner(partial_out.astype(jnp.bfloat16), "tensor", 1).astype(jnp.bfloat16)
    fisher = ((grad_hidden * gate_vals) ** 2).astype(jnp.bfloat16)
    fisher_vals = fisher.astype(jnp.float32)
    fisher_local = jnp.sum(fisher_vals)
    fisher_sum = by_axis(fisher_local, DP_TENSOR)
    weighted = (fisher_vals * residual).astype(jnp.bfloat16)
    recon_local = jnp.sum(fisher_vals * residual * residual)
    centered = 2.0 * soft_bits - 1.0
    reg_local = jnp.sum(1.0 - (centered * centered) ** 2)
    grad_sum = lax.psum_scatter(
        lax.dot_general(
            features, weighted, (((0,), (0,)), ((), ())), preferred_element_type=jnp.float32
        ).astype(jnp.bfloat16),
        DP,
        scatter_dimension=0,
        tiled=True,
    ).astype(jnp.float32)
    recon_total, reg_total = (by_axis(recon_local, DP_TENSOR), by_axis(reg_local, DP_TENSOR))
    total_cells = lax.axis_size(DP) * lax.axis_size("tensor") * tok_rows * ff_cols
    weight_cells = D * FFW
    fisher_mean = fisher_sum / total_cells
    sig_slope = soft_bits * (1.0 - soft_bits)
    grad_logit = (
        grad_sum * (2.0 / fisher_mean) * quant_step[None, :] * sig_slope
        - reg_weight * 8.0 * centered**3 * sig_slope
    )
    loss = recon_total / (fisher_mean * total_cells) + reg_weight * reg_total / weight_cells
    return (block_output, fisher, grad_logit, loss)


def solution(mesh):
    torus = Mesh(
        mesh.devices.reshape(4, 4, 2, mesh.shape["tensor"]), ("dp_0", "dp_1", "dp_2", "tensor")
    )
    in_specs = (
        P(DP, "tensor"),
        P(DP, "tensor"),
        P(DP, "tensor"),
        P(DP, "tensor"),
        P("tensor", DP),
        P("tensor"),
        P(DP, "tensor"),
        P(DP, "tensor"),
    )
    out_specs = (P(DP, "tensor"), P(DP, "tensor"), P(DP, "tensor"), P())
    return jax.shard_map(body, mesh=torus, in_specs=in_specs, out_specs=out_specs, check_vma=False)
```

profile of v0, /device:TPU:0, one launch (start us, length us, event | category | flops | bytes accessed | tf_op | source)
XLA Modules:
  0.0 318.8 jit_solution(8088553323695155464)
XLA Ops:
  7.2 0.0 copy-start
  7.2 0.0 copy-start.3
  7.2 0.0 copy-start.2
  7.2 0.0 copy-start.1
  7.2 0.0 copy-start.5
  7.2 0.0 all-gather.4.cloned.1.call-start
  7.3 2.4 pad_maximum_fusion
  9.6 0.0 all-gather.4.cloned.1.call-update
  9.6 0.0 all-gather.8.cloned.1.call-start
  9.7 0.7 all-gather.8.cloned.1.call-update
  10.4 0.0 all-gather.6.cloned.1.call-start
  10.4 0.0 copy-done
  10.5 0.0 copy-done.3
  10.5 0.0 copy-done.2
  10.5 0.9 fusion.26
  11.4 0.0 copy-done.1
  11.4 0.9 pad_maximum_fusion.1
  12.3 0.0 all-gather.6.cloned.1.call-update
  12.3 0.0 reduce-scatter.2.cloned.1.call-start
  12.4 46.4 %all-gather.4.cloned.1.call-done = bf16[768,2560]{1,0:T(8,128)(2,1)} async-done(((bf16[768,640]{1,0:T(8,128)(2,1)}), bf16[768,2560]{1,0:T(8,128)(2,1)}) %all-gather.4.cloned.1.call-update) | async-done | bytes 3932176 | tf_op jit(solution)/shard_map/all_gather | solution.py:20
  58.8 57.3 %all-gather.8.cloned.1.call-done = bf16[1728,2560]{0,1:T(8,128)(2,1)} async-done(((bf16[1728,80]{0,1:T(8,128)(2,1)}), bf16[1728,2560]{0,1:T(8,128)(2,1)}) %all-gather.8.cloned.1.call-update) | async-done | bytes 8847376 | tf_op jit(solution)/shard_map/all_gather | solution.py:56
  116.1 0.0 copy-done.5
  116.1 10.2 %fusion.9 = bf16[384,1728]{0,1:T(8,128)(2,1)} fusion(bf16[384,1728]{0,1:T(8,128)(2,1)S(1)} %copy-done.5, bf16[1728,2560]{0,1:T(8,128)(2,1)} %all-gather.8.cloned.1.call-done, bf16[768,2560]{1,0:T(8,128)(2,1)} %all-gather.4.cloned.1.call-done), kind=kOutput, calls=%fused_computation.13 | convolution fusion | flops 3400040448 | bytes 13795328 | tf_op jit(solution)/shard_map/dot_general | solution.py:58
  126.3 0.0 copy-start.6
  126.3 67.1 %all-gather.6.cloned.1.call-done = bf16[2560,3456]{1,0:T(8,128)(2,1)} async-done(((bf16[80,3456]{1,0:T(8,128)(2,1)}), bf16[2560,3456]{1,0:T(8,128)(2,1)}) %all-gather.6.cloned.1.call-update) | async-done | bytes 17694736 | tf_op jit(solution)/shard_map/all_gather | solution.py:20
  193.4 0.0 copy-start.4
  193.4 13.6 %fusion.13 = (f32[]{:T(128)}, f32[]{:T(128)}, f32[384,1728]{0,1:T(8,128)S(1)}) fusion(bf16[384,1728]{0,1:T(8,128)(2,1)} %fusion.9, bf16[2560,3456]{1,0:T(8,128)(2,1)} %all-gather.6.cloned.1.call-done, bf16[768,2560]{1,0:T(8,128)(2,1)} %all-gather.4.cloned.1.call-done), kind=kOutput, calls=%fused_computation.15 | convolution fusion | flops 3400704000 | bytes 15122440 | tf_op jit(solution)/shard_map/dot_general | solution.py:61
  206.9 0.0 copy-done.6
  206.9 0.0 copy-done.4
  207.0 7.4 %convolution_convert_fusion = bf16[2560,1728]{1,0:T(8,128)(2,1)} fusion(bf16[768,2560]{1,0:T(8,128)(2,1)S(1)} %copy-done.4, f32[384,1728]{0,1:T(8,128)S(1)} %get-tuple-element.20, bf16[384,1728]{0,1:T(8,128)(2,1)S(1)} %copy-done.6), kind=kOutput, calls=%fused_computation | convolution fusion | flops 3403800576 | bytes 14794752 | tf_op jit(solution)/shard_map/dot_general | solution.py:72
  214.4 0.0 reduce-scatter.2.cloned.1.call-update
  214.4 14.0 %convolution_convert_fusion.1 = bf16[384,2560]{1,0:T(8,128)(2,1)S(1)} fusion(bf16[1728,2560]{0,1:T(8,128)(2,1)} %all-gather.8.cloned.1.call-done, bf16[2560,3456]{1,0:T(8,128)(2,1)} %all-gather.6.cloned.1.call-done, bf16[384,1728]{0,1:T(8,128)(2,1)} %param.9, bf16[768,2560]{1,0:T(8,128)(2,1)} %all-gather.4.cloned.1.call-done), kind=kOutput, calls=%fused_computation.5 | convolution fusion | flops 6797746176 | bytes 23609344 | tf_op jit(solution)/shard_map/dot_general | solution.py:57
  228.5 1.4 copy.15
  229.9 4.2 %all-to-all-start = ((bf16[4,384,640]{2,1,0:T(8,128)(2,1)}), bf16[4,384,640]{2,1,0:T(8,128)(2,1)S(1)}, u32[]{:S(2)}, u32[]{:S(2)}) async-start(bf16[4,384,640]{2,1,0:T(8,128)(2,1)} %bitcast.9), calls=%async_computation | async-start | bytes 3932160 | tf_op jit(solution)/shard_map/all_to_all | solution.py:34
  234.2 10.7 %all-reduce.2 = (f32[]{:T(128)}, f32[]{:T(128)}, f32[]{:T(128)}) all-reduce(f32[]{:T(128)} %get-tuple-element.5, f32[]{:T(128)} %get-tuple-element.4, f32[]{:T(128)} %get-tuple-element.18), channel_id=1, replica_groups=mesh['dp_0'=4,'dp_1'=4,'dp_2'=2,'tensor'=4] {'dp_0'}, use_global_device_ids=true, to_apply=%region_3.0 | all-reduce | flops 3 | bytes 24 | tf_op jit(solution)/shard_map/psum | solution.py:39
  244.9 9.5 %all-reduce.1 = (f32[]{:T(128)}, f32[]{:T(128)}, f32[]{:T(128)}) all-reduce(f32[]{:T(128)} %get-tuple-element.12, f32[]{:T(128)} %get-tuple-element.13, f32[]{:T(128)} %get-tuple-element.14), channel_id=1, replica_groups=mesh['dp_0'=4,'dp_1'=4,'dp_2'=2,'tensor'=4] {'dp_1'}, use_global_device_ids=true, to_apply=%region_4.0 | all-reduce | flops 3 | bytes 24 | tf_op jit(solution)/shard_map/psum | solution.py:39
  254.4 3.1 all-reduce.3
  257.4 11.6 %all-reduce = (f32[]{:T(128)}, f32[]{:T(128)}, f32[]{:T(128)}) all-reduce(f32[]{:T(128)} %get-tuple-element.15, f32[]{:T(128)} %get-tuple-element.16, f32[]{:T(128)} %get-tuple-element.17), channel_id=1, replica_groups=mesh['dp_0'=4,'dp_1'=4,'dp_2'=2,'tensor'=4] {'tensor'}, use_global_device_ids=true, to_apply=%region_6.0 | all-reduce | flops 3 | bytes 24 | tf_op jit(solution)/shard_map/psum | solution.py:39
  271.7 0.0 all-to-all-done
  271.7 1.2 reduce_sum.39
  272.9 36.2 %reduce-scatter.2.cloned.1.call-done = bf16[80,1728]{1,0:T(8,128)(2,1)} async-done(((bf16[2560,1728]{1,0:T(8,128)(2,1)}), bf16[80,1728]{1,0:T(8,128)(2,1)}) %reduce-scatter.2.cloned.1.call-update) | async-done | bytes 276496 | tf_op jit(solution)/shard_map/reduce_scatter | solution.py:71
  309.1 2.1 fusion.24
Async XLA Ops:
  7.2 3.3 %copy-start = (f32[80,1728]{1,0:T(8,128)S(1)}, f32[80,1728]{1,0:T(8,128)}, u32[]{:S(2)}) copy-start(f32[80,1728]{1,0:T(8,128)} %param.14) | copy-start | bytes 1658884
  7.2 3.3 %copy-start.3 = (f32[1728]{0:T(1024)S(1)}, f32[1728]{0:T(1024)}, u32[]{:S(2)}) copy-start(f32[1728]{0:T(1024)} %param.13) | copy-start | bytes 20740
  7.2 3.3 %copy-start.2 = (bf16[80,1728]{1,0:T(8,128)(2,1)S(1)}, bf16[80,1728]{1,0:T(8,128)(2,1)}, u32[]{:S(2)}) copy-start(bf16[80,1728]{1,0:T(8,128)(2,1)} %param.15) | copy-start | bytes 829444
  7.2 4.2 %copy-start.1 = (bf16[80,1728]{1,0:T(8,128)(2,1)S(1)}, bf16[80,1728]{1,0:T(8,128)(2,1)}, u32[]{:S(2)}) copy-start(bf16[80,1728]{1,0:T(8,128)(2,1)} %param.11) | copy-start | bytes 829444
  7.2 108.9 %copy-start.5 = (bf16[384,1728]{0,1:T(8,128)(2,1)S(1)}, bf16[384,1728]{0,1:T(8,128)(2,1)}, u32[]{:S(2)}) copy-start(bf16[384,1728]{0,1:T(8,128)(2,1)} %param.9) | copy-start | bytes 3981316
  7.2 51.6 %all-gather.4.cloned.1.call-start = ((), (), s32[]{:S(2)}) async-start(), calls=%async_computation.2 | async-start | bytes 4915200 | tf_op jit(solution)/shard_map/all_gather | solution.py:20
  9.6 106.4 %all-gather.8.cloned.1.call-start = ((), (), s32[]{:S(2)}) async-start(), calls=%async_computation.4 | async-start | bytes 9461760 | tf_op jit(solution)/shard_map/all_gather | solution.py:56
  10.4 183.0 %all-gather.6.cloned.1.call-start = ((), (), s32[]{:S(2)}) async-start(), calls=%async_computation.3 | async-start | bytes 18247680 | tf_op jit(solution)/shard_map/all_gather | solution.py:20
  12.3 296.7 %reduce-scatter.2.cloned.1.call-start = ((), (), s32[]{:S(2)}) async-start(), calls=%async_computation.5 | async-start | bytes 9461760 | tf_op jit(solution)/shard_map/reduce_scatter | solution.py:71
  126.3 80.7 %copy-start.6 = (bf16[384,1728]{0,1:T(8,128)(2,1)S(1)}, bf16[384,1728]{0,1:T(8,128)(2,1)}, u32[]{:S(2)}) copy-start(bf16[384,1728]{0,1:T(8,128)(2,1)} %fusion.9) | copy-start | bytes 3981316
  193.4 13.6 %copy-start.4 = (bf16[768,2560]{1,0:T(8,128)(2,1)S(1)}, bf16[768,2560]{1,0:T(8,128)(2,1)}, u32[]{:S(2)}) copy-start(bf16[768,2560]{1,0:T(8,128)(2,1)} %all-gather.4.cloned.1.call-done) | copy-start | bytes 11796484
  229.9 41.8 %all-to-all-start = ((bf16[4,384,640]{2,1,0:T(8,128)(2,1)}), bf16[4,384,640]{2,1,0:T(8,128)(2,1)S(1)}, u32[]{:S(2)}, u32[]{:S(2)}) async-start(bf16[4,384,640]{2,1,0:T(8,128)(2,1)} %bitcast.9), calls=%async_computation | async-start | bytes 3932160 | tf_op jit(solution)/shard_map/all_to_all | solution.py:34
Sparse Core Ops, SparseCore 0:
  10.3 48.4 all-gather.3
  61.0 54.9 all-gather.7
  119.0 74.3 all-gather.5
  214.5 94.5 reduce-scatter.1
where the time goes:
time: 319 us
  waiting for transfers between devices  208 us (65%)
  matrix products  45.2 us (14%)
  blocking collectives  34.9 us (11%)
  between operations  17.7 us (6%)
  other arithmetic  7.47 us (2%)
  starting transfers between devices  4.41 us (1%)
    all_gather x2, waiting for transfers between devices, side_by_side(): whole, at, outs = (lax.all_gather(both, axis, axis=dim, tiled=True), 0, [])  113 us
    all_gather x1, waiting for transfers between devices, body(): down_full = lax.all_gather(down_weight, DP, axis=1, tiled=True)  57.3 us
    reduce_scatter x1, waiting for transfers between devices, body(): lax.psum_scatter(lax.dot_general(features, weighted, (((0,), (0,)), ((),...  36.2 us
    psum x4, blocking collectives, by_axis(): return functools.reduce(lax.psum, axes, array)  34.9 us
    dot_general x1, matrix products, body(): partial_out = jnp.dot(hidden, down_full, preferred_element_type=jnp.float32)  14 us
    dot_general x1, matrix products, body(): residual = jnp.dot(features, delta_full, preferred_element_type=jnp.float32)  13.6 us
    dot_general x1, matrix products, body(): lax.dot_general(out_grads, down_full, (((1,), (1,)), ((), ())), preferred...  10.2 us
    dot_general x1, matrix products, body(): lax.dot_general(features, weighted, (((0,), (0,)), ((), ())), preferred_e...  7.44 us
  transfers between devices with their start and end apart: 5, of which 4 were waited for; matrix products, arithmetic and copies ran while one was open for 9% of the time, Pallas kernels for 0%

commit v1 on v0

v1 whole, which is shorter than its diff:
```python
import jax
import jax.numpy as jnp
from jax import lax
from jax.experimental import pallas as pl
from jax.experimental.pallas import tpu as pltpu
from jax.sharding import Mesh
from jax.sharding import PartitionSpec as P

D = 2560
FFW = 6912
TOK = 384
FF = 1728
FFP = 1792
ROWS = 80
XW = 640
TILE = 256
NT = FFP // TILE
REG_WEIGHT = 0.5
BF = jnp.bfloat16
F32 = jnp.float32
MESH = pl.DeviceIdType.MESH

GATHER = (("y", "z", 1), ("z", "y", 1), ("y", "z", -1), ("z", "y", -1))
REDUCE = (("z", "y", 1), ("y", "z", 1), ("z", "y", -1), ("y", "z", -1))
COLS = ((0, 512), (512, 512), (1024, 384), (1408, 384))
GATHER_COLS = ((0, 1, 2, 3), (2, 3, 0, 1), (0, 1, 2, 3))
REDUCE_COLS = (2, 3, 0, 1)
SUBS = 3
SUB_ROWS = TOK // 2 // SUBS


def kernel(
    w_in, bi, go, gate_in, reg_in,
    block_out, fisher_out, gsum, stats,
    full, xf, feats_t, gate, fish, wbuf, grad, pair, ring, outp, outr, reg, acc, stat,
    local, ag_recv, ag_send, pr_recv, pr_send, x_recv, x_send,
    rs_recv, rs_send, pe_recv, pe_send, xo_recv, xo_send, st_recv, st_send,
):
    me = {name: lax.axis_index(name) for name in ("z", "y", "c", "x")}
    z, y, c, x = me["z"], me["y"], me["c"], me["x"]
    other = {"c": 1 - c}

    def at(axis, k):
        return lax.rem(me[axis] + (k + 4), 4)

    def step_to(axis, sign):
        return {axis: at(axis, sign)}

    def remote(src, dst, send, recv, device):
        return pltpu.make_async_remote_copy(
            src_ref=src, dst_ref=dst, send_sem=send, recv_sem=recv, device_id=device, device_id_type=MESH
        )

    def back(axis, sign, k):
        return lax.rem(me[axis] + (4 - k if sign > 0 else k), 4)

    def ahead(axis, sign, k):
        return lax.rem(me[axis] + (k if sign > 0 else 4 - k), 4)

    def cols_of(a, s):
        lo, width = COLS[GATHER_COLS[a][s]]
        return pl.ds(lo, width)

    def piece(a, s, d, e):
        first, second, sign = GATHER[s]
        co = {first: back(first, sign, d), second: back(second, sign, e)}
        return full.at[a, co["z"], co["y"], c, :, cols_of(a, s)]

    def send_first(a, s, d):
        first, second, sign = GATHER[s]
        ref = piece(a, s, d, 0)
        remote(ref, ref, ag_send.at[a, s], ag_recv.at[a, s, d + 1], step_to(first, sign)).start()

    def send_second(a, s, d, e):
        first, second, sign = GATHER[s]
        ref = piece(a, s, d, e)
        remote(ref, ref, ag_send.at[a, s], ag_recv.at[a, s, (e + 1) * 4 + d], step_to(second, sign)).start()

    def wait_piece(a, s, d, e):
        ref = piece(a, s, d, e)
        remote(ref, ref, ag_send.at[a, s], ag_recv.at[a, s, e * 4 + d], other).wait_recv()

    def bundle(a, s, e, parity):
        first, second, sign = GATHER[s]
        g = back(second, sign, e)
        if second == "z":
            return full.at[a, g, :, parity, :, cols_of(a, s)]
        return full.at[a, :, g, parity, :, cols_of(a, s)]

    def send_pair(a, s, e):
        ref = bundle(a, s, e, c)
        remote(ref, ref, pr_send.at[a, s], pr_recv.at[a, s, e], other).start()

    def ag_start(a):
        for s in range(4):
            send_first(a, s, 0)
            send_second(a, s, 0, 0)

    def ag_first(a, d):
        for s in range(4):
            wait_piece(a, s, d, 0)
            if d < 3:
                send_first(a, s, d)
            send_second(a, s, d, 0)
            if d == 3:
                send_pair(a, s, 0)

    def ag_second(a, k):
        e, d = 1 + k // 4, lax.rem(k, 4)
        for s in range(4):
            wait_piece(a, s, d, e)

            @pl.when(e < 3)
            def _():
                send_second(a, s, d, e)

            @pl.when(d == 3)
            def _():
                send_pair(a, s, e)

    def ag_finish(a):
        for s in range(4):
            for e in range(4):
                ref = bundle(a, s, e, 1 - c)
                remote(ref, ref, pr_send.at[a, s], pr_recv.at[a, s, e], other).wait_recv()

    def ag_drain(a):
        for s in range(4):
            ref = ring.at[:, :, cols_of(a, s)]
            remote(ref, ref, ag_send.at[a, s], ag_recv.at[a, s, 0], other).wait_send()
            ref = full.at[a, :, :, c, :, cols_of(a, s)]
            remote(ref, ref, pr_send.at[a, s], pr_recv.at[a, s, 0], other).wait_send()

    def x_block(t, k, lo, count):
        return xf.at[t, pl.ds(lo, count), pl.ds(pl.multiple_of(at("x", k) * XW, XW), XW)]

    X_MOVES = ((0, 1, 0, TOK, -1), (0, -1, 0, TOK, 1), (-1, 1, 0, TOK // 2, 2), (1, -1, TOK // 2, TOK // 2, 2))

    def x_copy(t, i, k):
        src, sign, lo, count, got = X_MOVES[i]
        ref = x_block(t, k, lo, count)
        return remote(ref, ref, x_send.at[t, i], x_recv.at[t, i], step_to("x", sign))

    def x_start(t, i):
        x_copy(t, i, X_MOVES[i][0]).start()

    def x_wait(t, i):
        x_copy(t, i, X_MOVES[i][4]).wait_recv()

    def r_cols(s):
        lo, width = COLS[REDUCE_COLS[s]]
        return pl.ds(lo, width)

    def pair_copy(s):
        return remote(
            grad.at[:, :, 1 - c, :, r_cols(s)], pair.at[:, :, :, r_cols(s)], pe_send.at[s], pe_recv.at[s], other
        )

    def ring_copy(s, src, slot, device):
        return remote(src, ring.at[slot, :, r_cols(s)], rs_send.at[s], rs_recv.at[s, slot], device)

    def rs_step(s, t, j):
        first, second, sign = REDUCE[s]
        cols = r_cols(s)
        co = {first: ahead(first, sign, 3 - t), second: ahead(second, sign, 3 - j)}
        mine = grad.at[co["z"], co["y"], c, :, cols]
        total = mine[...].astype(F32) + pair[co["z"], co["y"], :, cols].astype(F32)

        def arrived(slot):
            ring_copy(s, mine, slot, other).wait_recv()
            return ring[slot, :, cols].astype(F32)

        if t > 0:
            total = total + arrived((t - 1) * 4 + j)
        if t < 3:
            mine[...] = total.astype(BF)
            ring_copy(s, mine, t * 4 + j, step_to(first, sign)).start()
            return
        if j > 0:
            total = total + arrived(12 + j - 1)
        if j < 3:
            mine[...] = total.astype(BF)
            ring_copy(s, mine, 12 + j, step_to(second, sign)).start()
        else:
            gsum[:, cols] = total

    def xo_rows(way, sub):
        return pl.ds(way * (TOK // 2) + sub * SUB_ROWS, SUB_ROWS)

    def xo_copy(way, sub, t):
        sign = 1 - 2 * way
        rows = xo_rows(way, sub)
        return remote(
            outp.at[ahead("x", sign, 3 - t), rows, :], outr.at[t, rows, :],
            xo_send.at[way, sub, t], xo_recv.at[way, sub, t], step_to("x", sign),
        )

    def xo_step(way, sub, t):
        sign = 1 - 2 * way
        rows = xo_rows(way, sub)
        if t > 0:
            own = ahead("x", sign, 3 - t)
            xo_copy(way, sub, t - 1).wait_recv()
            total = outp[own, rows, :].astype(F32) + outr[t - 1, rows, :].astype(F32)
            if t == 3:
                block_out[rows, :] = total.astype(BF)
                return
            outp[own, rows, :] = total.astype(BF)
        xo_copy(way, sub, t).start()

    ST_AXES = (("y", 4), ("z", 4), ("x", 4), ("c", 2))

    def st_copy(ph, slot, k):
        axis, size = ST_AXES[ph]
        device = {axis: lax.rem(me[axis] + k, size)}
        ref = stat.at[ph, slot]
        return remote(ref, ref, st_send.at[ph, k], st_recv.at[ph, slot], device)

    def st_start(ph, total):
        axis, size = ST_AXES[ph]
        stat[ph, me[axis]] = total
        for k in range(1, size):
            st_copy(ph, me[axis], k).start()

    def st_finish(ph):
        axis, size = ST_AXES[ph]
        for k in range(1, size):
            st_copy(ph, lax.rem(me[axis] + k, size), k).wait_recv()
        total = stat[ph, 0]
        for k in range(1, size):
            total = total + stat[ph, k]
        return total

    def tile(n):
        return pl.ds(pl.multiple_of(n * TILE, TILE), TILE)

    def weights(a, n):
        return full[a, :, :, :, :, tile(n)].reshape(D, TILE)

    def fold(v):
        v = jnp.sum(v.reshape(TOK // 8, 8, TILE), axis=0)
        return v[:, :128] + v[:, 128:]

    def fisher_tile(n):
        product = jnp.dot(xf[0], weights(0, n), preferred_element_type=F32)
        value = ((product * gate[:, tile(n)].astype(F32)) ** 2).astype(BF)
        fish[:, tile(n)] = value
        acc[0] += fold(value.astype(F32))

    def residual_tile(n):
        residual = jnp.dot(xf[1], weights(1, n), preferred_element_type=F32)
        weighted = fish[:, tile(n)].astype(F32) * residual
        wbuf[:, tile(n)] = weighted.astype(BF)
        acc[1] += fold(weighted * residual)

    def grad_tile(n):
        right = wbuf[:, tile(n)]
        for part in range(4):
            product = jnp.dot(feats_t[part], right, preferred_element_type=F32)
            grad[part, :, :, :, tile(n)] = product.astype(BF).reshape(4, 2, ROWS, TILE)

    def hidden_tile(n):
        product = jnp.dot(xf[1], weights(2, n), preferred_element_type=F32)
        wbuf[:, tile(n)] = (product * gate[:, tile(n)].astype(F32)).astype(BF)

    def out_tile(i):
        target = at("x", 3 - 2 * i + (i // 2) * 3)
        right = full[0, target].reshape(XW, FFP)
        product = lax.dot_general(wbuf[...], right, (((1,), (1,)), ((), ())), preferred_element_type=F32)
        outp[target] = product.astype(BF)

    own_cols = pl.ds(pl.multiple_of(x * XW, XW), XW)
    loads = [pltpu.make_async_copy(w_in.at[a], full.at[a, z, y, c], local.at[a]) for a in range(3)]
    loads += [
        pltpu.make_async_copy(go, xf.at[0, :, own_cols], local.at[3]),
        pltpu.make_async_copy(bi, xf.at[1, :, own_cols], local.at[4]),
        pltpu.make_async_copy(gate_in, gate, local.at[5]),
        pltpu.make_async_copy(reg_in, reg, local.at[6]),
    ]
    for load in loads:
        load.start()
    barrier = pltpu.get_barrier_semaphore()
    partners = [{axis: at(axis, k)} for axis in ("z", "y", "x") for k in (1, 2, 3)] + [other]
    for device in partners:
        pl.semaphore_signal(barrier, inc=1, device_id=device, device_id_type=MESH)
    acc[...] = jnp.zeros_like(acc)
    pl.semaphore_wait(barrier, len(partners))
    for load in loads:
        load.wait()

    for i in (0, 1):
        x_start(0, i)
    ag_start(0)
    for i in (0, 1):
        x_start(1, i)
    ag_start(1)
    for d in (1, 2, 3):
        ag_first(0, d)
    for i in (0, 1):
        x_wait(0, i)
    for i in (2, 3):
        x_start(0, i)

    @pl.loop(0, 12)
    def _(k):
        ag_second(0, k)

    ag_start(2)
    for d in (1, 2, 3):
        ag_first(1, d)
    for i in (2, 3):
        x_wait(0, i)
    for i in (0, 1):
        x_wait(1, i)
    for i in (2, 3):
        x_start(1, i)
    ag_finish(0)

    @pl.loop(0, NT)
    def _(n):
        @pl.when(n < 6)
        def _():
            ag_second(1, 2 * n)
            ag_second(1, 2 * n + 1)

        fisher_tile(n)

    save_fisher = pltpu.make_async_copy(fish, fisher_out, local.at[7])
    save_fisher.start()
    for i in (2, 3):
        x_wait(1, i)
    for part in range(4):
        feats_t[part] = jnp.transpose(xf[1, :, part * XW:(part + 1) * XW])
        if part < 3:
            ag_first(2, part + 1)
    ag_finish(1)

    @pl.loop(0, NT)
    def _(n):
        @pl.when(n < 6)
        def _():
            ag_second(2, 2 * n)
            ag_second(2, 2 * n + 1)

        residual_tile(n)
        grad_tile(n)
        for s in range(4):
            lo, width = COLS[REDUCE_COLS[s]]

            @pl.when(n == (lo + width - 1) // TILE)
            def _():
                pair_copy(s).start()

    acc[2] = reg[...]
    st_start(0, acc[...])
    by_ready = sorted(range(4), key=lambda s: REDUCE_COLS[s])
    for s in by_ready:
        pair_copy(s).wait_recv()

        @pl.loop(0, 4)
        def _(j):
            rs_step(s, 0, j)

    st_start(1, st_finish(0))
    ag_finish(2)

    @pl.loop(0, NT)
    def _(n):
        hidden_tile(n)

        @pl.when(n < 4)
        def _():
            for s in range(4):
                rs_step(s, 1, n)

        @pl.when(n >= 4)
        def _():
            for s in range(4):
                rs_step(s, 2, n - 4)

    for s in range(4):
        rs_step(s, 2, 3)
    st_start(2, st_finish(1))

    @pl.loop(0, 4)
    def _(i):
        out_tile(i)
        for way in range(2):
            @pl.when(i == way)
            def _():
                for sub in range(SUBS):
                    xo_step(way, sub, 0)

    st_start(3, st_finish(2))
    for t in (1, 2, 3):
        for s in range(4):
            rs_step(s, 3, t - 1)
        for sub in range(SUBS):
            for way in range(2):
                xo_step(way, sub, t)
    for s in range(4):
        rs_step(s, 3, 3)
    stats[...] = st_finish(3)

    for a in range(3):
        ag_drain(a)
    for t in range(2):
        for i in range(4):
            x_copy(t, i, X_MOVES[i][0]).wait_send()
    for s in range(4):
        pair_copy(s).wait_send()
        ref = ring.at[:, :, r_cols(s)]
        remote(ref, ref, rs_send.at[s], rs_recv.at[s, 0], other).wait_send()
    for way in range(2):
        for sub in range(SUBS):
            for t in range(3):
                xo_copy(way, sub, t).wait_send()
    for ph in range(4):
        for k in range(1, ST_AXES[ph][1]):
            st_copy(ph, me[ST_AXES[ph][0]], k).wait_send()
    save_fisher.wait()


def run(w_in, bi, go, gate_in, reg_in):
    vmem, hbm = pl.BlockSpec(memory_space=pltpu.VMEM), pl.BlockSpec(memory_space=pl.ANY)
    dma = pltpu.SemaphoreType.DMA
    return pl.pallas_call(
        kernel,
        out_shape=(
            jax.ShapeDtypeStruct((TOK, XW), BF),
            jax.ShapeDtypeStruct((TOK, FFP), BF),
            jax.ShapeDtypeStruct((ROWS, FFP), F32),
            jax.ShapeDtypeStruct((3, 8, 128), F32),
        ),
        in_specs=[hbm] * 5,
        out_specs=(vmem, hbm, vmem, vmem),
        scratch_shapes=[
            pltpu.VMEM((3, 4, 4, 2, ROWS, FFP), BF),
            pltpu.VMEM((2, TOK, D), BF),
            pltpu.VMEM((4, XW, TOK), BF),
            pltpu.VMEM((TOK, FFP), BF),
            pltpu.VMEM((TOK, FFP), BF),
            pltpu.VMEM((TOK, FFP), BF),
            pltpu.VMEM((4, 4, 2, ROWS, FFP), BF),
            pltpu.VMEM((4, 4, ROWS, FFP), BF),
            pltpu.VMEM((15, ROWS, FFP), BF),
            pltpu.VMEM((4, TOK, XW), BF),
            pltpu.VMEM((3, TOK, XW), BF),
            pltpu.VMEM((8, 128), F32),
            pltpu.VMEM((3, 8, 128), F32),
            pltpu.VMEM((4, 4, 3, 8, 128), F32),
            dma((8,)),
            dma((3, 4, 16)), dma((3, 4)), dma((3, 4, 4)), dma((3, 4)),
            dma((2, 4)), dma((2, 4)),
            dma((4, 16)), dma((4,)), dma((4,)), dma((4,)),
            dma((2, SUBS, 3)), dma((2, SUBS, 3)),
            dma((4, 4)), dma((4, 4)),
        ],
        compiler_params=pltpu.CompilerParams(
            collective_id=0, has_side_effects=True, vmem_limit_bytes=67043328
        ),
    )(w_in, bi, go, gate_in, reg_in)


def wide(a):
    return jnp.pad(a, ((0, 0), (0, FFP - FF)))


def body(
    block_input, gate_act, grad_out, up_weight, down_weight, quant_step, round_logit, grid_offset
):
    soft_bits = jax.nn.sigmoid(round_logit)
    weight_delta = (quant_step[None, :] * (soft_bits - grid_offset.astype(F32))).astype(BF)
    centered = 2.0 * soft_bits - 1.0
    reg_local = jnp.sum(1.0 - (centered * centered) ** 2)
    w_in = jnp.stack([wide(down_weight.T), wide(weight_delta), wide(up_weight)])
    reg_in = jnp.full((8, 128), reg_local * (1.0 / 1024.0), F32)
    block_output, fisher, grad_sum, stats = run(w_in, block_input, grad_out, wide(gate_act), reg_in)
    fisher_sum, recon_total, reg_total = (jnp.sum(stats[i]) for i in range(3))
    total_cells = 12288 * FFW
    weight_cells = D * FFW
    fisher_mean = fisher_sum / total_cells
    sig_slope = soft_bits * (1.0 - soft_bits)
    grad_logit = (
        grad_sum[:, :FF] * (2.0 / fisher_mean) * quant_step[None, :] * sig_slope
        - REG_WEIGHT * 8.0 * centered**3 * sig_slope
    )
    loss = recon_total / (fisher_mean * total_cells) + REG_WEIGHT * reg_total / weight_cells
    return (block_output, fisher[:, :FF], grad_logit, loss)


def solution(mesh):
    torus = Mesh(mesh.devices.reshape(4, 4, 2, 4), ("z", "y", "c", "x"))
    dp = ("z", "y", "c")
    in_specs = (
        P(dp, "x"), P(dp, "x"), P(dp, "x"), P(dp, "x"), P("x", dp), P("x"), P(dp, "x"), P(dp, "x"),
    )
    out_specs = (P(dp, "x"), P(dp, "x"), P(dp, "x"), P())
    return jax.shard_map(body, mesh=torus, in_specs=in_specs, out_specs=out_specs, check_vma=False)
```

time: 319 us -> 161 us (0.50)
  waiting for transfers between devices: 208 us -> 0 us
  Pallas kernels: 0 us -> 141 us
  matrix products: 45.2 us -> 0 us
  blocking collectives: 34.9 us -> 0 us
  between operations: 17.7 us -> 5.18 us
  local copies, waits for them, and re-layouts: 1.48 us -> 8.58 us
  starting transfers between devices: 4.41 us -> 0 us
    all_gather x3 -> x0, waiting for transfers between devices: 171 us -> none  [the longest x2 113 us: side_by_side(): whole, at, outs = (lax.all_gather(both, axis, axis=dim, tiled=True), 0, [])]
    pallas_call x0 -> x1, Pallas kernels: none -> 141 us  [run(): pl.pallas_call(kernel, out_shape=(jax.ShapeDtypeStruct((TOK, XW), BF), ja...]
    dot_general x4 -> x0, matrix products: 45.2 us -> none  [the longest x1 14 us: body(): partial_out = jnp.dot(hidden, down_full, preferred_element_type=jnp.float32)]
    reduce_scatter x1 -> x0, waiting for transfers between devices: 36.2 us -> none  [body(): lax.psum_scatter(lax.dot_general(features, weighted, (((0,), (0,)), ((),...]
    psum x4 -> x0, blocking collectives: 34.9 us -> none  [by_axis(): return functools.reduce(lax.psum, axes, array)]
    unnamed x14 -> x17, local copies, waits for them, and re-layouts: 0.03 us -> 5.72 us
    all_to_all x1 -> x0, starting transfers between devices: 4.25 us -> none  [sum_at_owner(): tiles = lax.all_to_all(in_blocks(array, dim, count), axis, 0, 0, tiled=True)]
    concatenate x2 -> x0, other arithmetic: 3.31 us -> none  [side_by_side(): both = jnp.concatenate(arrays, axis=along)]
  transfers between devices with their start and end apart: 5 -> 0, of which waited for: 4 -> 0; matrix products, arithmetic and copies ran while one was open for 9% -> 0% of each run, Pallas kernels for 0% -> 0%
where the time goes in v1:
time: 161 us; the launch traced here: 160 us
  Pallas kernels  141 us (88%)
  local copies, waits for them, and re-layouts  8.58 us (5%)
  between operations  5.18 us (3%)
  other arithmetic  4.76 us (3%)
    pallas_call x1, Pallas kernels, run(): pl.pallas_call(kernel, out_shape=(jax.ShapeDtypeStruct((TOK, XW), BF), ja...  141 us
    unnamed x17, local copies, waits for them, and re-layouts  5.72 us

profile of v1, /device:TPU:0, one launch (start us, length us, event | category | flops | bytes accessed | tf_op | source)
XLA Modules:
  0.0 159.9 jit_solution(3645261109788419646)
XLA Ops:
  0.6 0.0 copy-start.4
  0.6 1.0 pad_bitcast_fusion.2
  1.7 2.0 %fusion.1 = (f32[]{:T(128)}, bf16[80,1728]{1,0:T(8,128)(2,1)S(1)}) fusion(f32[80,1728]{1,0:T(8,128)} %param.14, bf16[80,1728]{1,0:T(8,128)(2,1)} %param.15, f32[1728]{0:T(1024)} %param.13), kind=kLoop, calls=%fused_computation.5 | loop fusion | flops 1797119 | bytes 1112836 | tf_op jit(solution)/shard_map/reduce_sum | solution.py:475
  4.4 0.6 broadcast_in_dim.2.reg_in
  4.9 0.0 copy-done.4
  5.0 0.0 copy-start.1
  5.0 0.1 pad_bitcast_fusion
  5.0 1.0 pad_maximum_fusion.w_in
  6.0 0.6 copy-done.1
  6.6 1.7 %copy.12 = bf16[384,1728]{1,0:T(8,128)(2,1)S(1)} copy(bf16[384,1728]{0,1:T(8,128)(2,1)S(1)} %copy-done.1) | data formatting | bytes 2654208 | tf_op args[1]
  8.3 1.2 pad.17.gate_in
  9.5 141.4 %shard_map.111 = (bf16[384,640]{1,0:T(8,128)(2,1)}, bf16[384,1792]{1,0:T(8,128)(2,1)}, f32[80,1792]{1,0:T(8,128)}, f32[3,8,128]{2,1,0:T(8,128)}) custom-call(bf16[3,80,1792]{2,1,0:T(8,128)(2,1)} %pad_maximum_fusion.w_in, bf16[384,640]{1,0:T(8,128)(2,1)} %bi.1, bf16[384,640]{1,0:T(8,128)(2,1)} %go.1, bf16[384,1792]{1,0:T(8,128)(2,1)} %pad.17.gate_in, ...), custom_call_target="tpu_custom_call" | custom-call | tf_op jit(solution)/shard_map/pallas_call | solution.py:427
  151.0 0.0 copy-start.6
  151.0 0.0 copy-start
  151.0 0.0 copy-start.2
  151.0 0.0 copy-start.5
  151.0 2.6 %copy.13 = bf16[384,1728]{0,1:T(8,128)(2,1)} copy(bf16[384,1728]{1,0:T(8,128)(2,1)} %bitcast.8) | data formatting | bytes 2654208
  153.6 0.0 copy-done.6
  153.6 0.0 copy-start.3
  153.6 0.6 slice_reduce_fusion
  156.9 0.0 copy-done
  156.9 0.0 copy-done.2
  156.9 0.0 copy-done.5
  156.9 1.1 fusion.4
  158.0 0.0 copy-done.3
  158.0 0.8 copy.15
Async XLA Ops:
  0.6 4.3 %copy-start.4 = (bf16[80,1728]{1,0:T(8,128)(2,1)S(1)}, bf16[80,1728]{1,0:T(8,128)(2,1)}, u32[]{:S(2)}) copy-start(bf16[80,1728]{1,0:T(8,128)(2,1)} %param.11) | copy-start | bytes 829444
  5.0 1.6 %copy-start.1 = (bf16[384,1728]{0,1:T(8,128)(2,1)S(1)}, bf16[384,1728]{0,1:T(8,128)(2,1)}, u32[]{:S(2)}) copy-start(bf16[384,1728]{0,1:T(8,128)(2,1)} %param.9) | copy-start | bytes 3981316
  151.0 2.6 %copy-start.6 = (f32[3,8,128]{2,1,0:T(8,128)S(1)}, f32[3,8,128]{2,1,0:T(8,128)}, u32[]{:S(2)}) copy-start(f32[3,8,128]{2,1,0:T(8,128)} %get-tuple-element.11) | copy-start | bytes 36868
  151.0 5.9 %copy-start = (f32[80,1728]{1,0:T(8,128)S(1)}, f32[80,1728]{1,0:T(8,128)}, u32[]{:S(2)}) copy-start(f32[80,1728]{1,0:T(8,128)} %param.14) | copy-start | bytes 1658884
  151.0 5.9 %copy-start.2 = (f32[80,1792]{1,0:T(8,128)S(1)}, f32[80,1792]{1,0:T(8,128)}, u32[]{:S(2)}) copy-start(f32[80,1792]{1,0:T(8,128)} %get-tuple-element.10) | copy-start | bytes 1720324
  151.0 5.9 %copy-start.5 = (f32[1728]{0:T(1024)S(1)}, f32[1728]{0:T(1024)}, u32[]{:S(2)}) copy-start(f32[1728]{0:T(1024)} %param.13) | copy-start | bytes 20740
  153.6 4.4 %copy-start.3 = (bf16[384,640]{1,0:T(8,128)(2,1)S(1)}, bf16[384,640]{1,0:T(8,128)(2,1)}, u32[]{:S(2)}) copy-start(bf16[384,640]{1,0:T(8,128)(2,1)} %get-tuple-element.27) | copy-start | bytes 1474564

commit v2 on v1

v2 whole, which is shorter than its diff:
```python
import jax
import jax.numpy as jnp
from jax import lax
from jax.experimental import pallas as pl
from jax.experimental.pallas import tpu as pltpu
from jax.sharding import Mesh
from jax.sharding import PartitionSpec as P

D = 2560
FFW = 6912
TOK = 384
FF = 1728
FFP = 1792
ROWS = 80
XW = 640
TILE = 256
NT = FFP // TILE
REG_WEIGHT = 0.5
CELLS = 12288 * FFW
WEIGHT_CELLS = D * FFW
BF = jnp.bfloat16
F32 = jnp.float32
MESH = pl.DeviceIdType.MESH

GATHER = (("y", "z", 1), ("z", "y", 1), ("y", "z", -1), ("z", "y", -1), ("z", "y", -1))
REDUCE = tuple((second, first, sign) for first, second, sign in GATHER)
PARTS = ((0, 48, 0, 768), (0, 48, 768, 768), (48, 32, 0, 1152), (0, 48, 1536, 256), (48, 32, 1152, 640))
STREAMS = len(PARTS)
READY = tuple((col + cols - 1) // TILE for _, _, col, cols in PARTS)
EARLY = tuple(s for s in range(STREAMS) if READY[s] < NT - 1)
LATE = tuple(s for s in range(STREAMS) if READY[s] == NT - 1)
SUBS = 3
SUB_ROWS = TOK // 2 // SUBS


def kernel(
    bi, gate_in, go, up_in, down_in, step_in, logit_in, offset_in,
    block_out, fisher_out, grad_logit, loss_out,
    full, xf, feats_t, gate, gate_t, fish, wbuf, grad, pair, ring, outp, outr, acc, stat,
    up_own, down_own, step_own, logit, offset, slope, pull, gsum,
    local, ag_recv, ag_send, pr_recv, pr_send, x_recv, x_send,
    rs_recv, rs_send, pe_recv, pe_send, xo_recv, xo_send, st_recv, st_send,
):
    me = {name: lax.axis_index(name) for name in ("z", "y", "c", "x")}
    z, y, c, x = me["z"], me["y"], me["c"], me["x"]
    other = {"c": 1 - c}

    def at(axis, k):
        return lax.rem(me[axis] + (k + 4), 4)

    def step_to(axis, sign):
        return {axis: at(axis, sign)}

    def remote(src, dst, send, recv, device):
        return pltpu.make_async_remote_copy(
            src_ref=src, dst_ref=dst, send_sem=send, recv_sem=recv, device_id=device, device_id_type=MESH
        )

    def back(axis, sign, k):
        return lax.rem(me[axis] + (4 - k if sign > 0 else k), 4)

    def ahead(axis, sign, k):
        return lax.rem(me[axis] + (k if sign > 0 else 4 - k), 4)

    def part(s):
        row, rows, col, cols = PARTS[s]
        return pl.ds(row, rows), pl.ds(col, cols)

    def piece(a, s, d, e):
        first, second, sign = GATHER[s]
        co = {first: back(first, sign, d), second: back(second, sign, e)}
        return full.at[a, co["z"], co["y"], c, *part(s)]

    def send_first(a, s, d):
        first, second, sign = GATHER[s]
        ref = piece(a, s, d, 0)
        remote(ref, ref, ag_send.at[a, s], ag_recv.at[a, s, d + 1], step_to(first, sign)).start()

    def send_second(a, s, d, e):
        first, second, sign = GATHER[s]
        ref = piece(a, s, d, e)
        remote(ref, ref, ag_send.at[a, s], ag_recv.at[a, s, (e + 1) * 4 + d], step_to(second, sign)).start()

    def wait_piece(a, s, d, e):
        ref = piece(a, s, d, e)
        remote(ref, ref, ag_send.at[a, s], ag_recv.at[a, s, e * 4 + d], other).wait_recv()

    def bundle(a, s, e, parity):
        first, second, sign = GATHER[s]
        g = back(second, sign, e)
        if second == "z":
            return full.at[a, g, :, parity, *part(s)]
        return full.at[a, :, g, parity, *part(s)]

    def send_pair(a, s, e):
        ref = bundle(a, s, e, c)
        remote(ref, ref, pr_send.at[a, s], pr_recv.at[a, s, e], other).start()

    def ag_start(a):
        for s in range(STREAMS):
            send_first(a, s, 0)
            send_second(a, s, 0, 0)

    def ag_first(a, d):
        for s in range(STREAMS):
            wait_piece(a, s, d, 0)

            @pl.when(d < 3)
            def _():
                send_first(a, s, d)

            send_second(a, s, d, 0)

            @pl.when(d == 3)
            def _():
                send_pair(a, s, 0)

    def ag_second(a, k):
        e, d = 1 + k // 4, k % 4
        for s in range(STREAMS):
            wait_piece(a, s, d, e)

            @pl.when(e < 3)
            def _():
                send_second(a, s, d, e)

            @pl.when(d == 3)
            def _():
                send_pair(a, s, e)

    def ag_finish(a):
        for s in range(STREAMS):
            for e in range(4):
                ref = bundle(a, s, e, 1 - c)
                remote(ref, ref, pr_send.at[a, s], pr_recv.at[a, s, e], other).wait_recv()

    def ag_drain(a):
        for s in range(STREAMS):
            ref = ring.at[:, *part(s)]
            remote(ref, ref, ag_send.at[a, s], ag_recv.at[a, s, 0], other).wait_send()
            ref = full.at[a, :, :, c, *part(s)]
            remote(ref, ref, pr_send.at[a, s], pr_recv.at[a, s, 0], other).wait_send()

    def x_block(t, k, lo, count):
        return xf.at[t, pl.ds(lo, count), pl.ds(pl.multiple_of(at("x", k) * XW, XW), XW)]

    X_MOVES = ((0, 1, 0, TOK, -1), (0, -1, 0, TOK, 1), (-1, 1, 0, TOK // 2, 2), (1, -1, TOK // 2, TOK // 2, 2))

    def x_copy(t, i, k):
        src, sign, lo, count, got = X_MOVES[i]
        ref = x_block(t, k, lo, count)
        return remote(ref, ref, x_send.at[t, i], x_recv.at[t, i], step_to("x", sign))

    def x_start(t, i):
        x_copy(t, i, X_MOVES[i][0]).start()

    def x_wait(t, i):
        x_copy(t, i, X_MOVES[i][4]).wait_recv()

    def pair_copy(s):
        return remote(
            grad.at[:, :, 1 - c, *part(s)], pair.at[:, :, *part(s)], pe_send.at[s], pe_recv.at[s], other
        )

    def ring_copy(s, src, slot, device):
        return remote(src, ring.at[slot, *part(s)], rs_send.at[s], rs_recv.at[s, slot], device)

    def rs_step(s, t, j):
        first, second, sign = REDUCE[s]
        co = {first: ahead(first, sign, 3 - t), second: ahead(second, sign, 3 - j)}
        mine = grad.at[co["z"], co["y"], c, *part(s)]
        total = mine[...].astype(F32) + pair[co["z"], co["y"], *part(s)].astype(F32)

        def arrived(slot):
            ring_copy(s, mine, slot, other).wait_recv()
            return ring[slot, *part(s)].astype(F32)

        if t > 0:
            total = total + arrived((t - 1) * 4 + j)
        if t < 3:
            mine[...] = total.astype(BF)
            ring_copy(s, mine, t * 4 + j, step_to(first, sign)).start()
            return
        if j > 0:
            total = total + arrived(12 + j - 1)
        if j < 3:
            mine[...] = total.astype(BF)
            ring_copy(s, mine, 12 + j, step_to(second, sign)).start()
        else:
            gsum[*part(s)] = total

    def xo_rows(way, sub):
        return pl.ds(way * (TOK // 2) + sub * SUB_ROWS, SUB_ROWS)

    def xo_copy(way, sub, t):
        sign = 1 - 2 * way
        rows = xo_rows(way, sub)
        return remote(
            outp.at[ahead("x", sign, 3 - t), rows, :], outr.at[t, rows, :],
            xo_send.at[way, sub, t], xo_recv.at[way, sub, t], step_to("x", sign),
        )

    def xo_step(way, sub, t):
        sign = 1 - 2 * way
        rows = xo_rows(way, sub)
        if t > 0:
            own = ahead("x", sign, 3 - t)
            xo_copy(way, sub, t - 1).wait_recv()
            total = outp[own, rows, :].astype(F32) + outr[t - 1, rows, :].astype(F32)
            if t == 3:
                block_out[rows, :] = total.astype(BF)
                return
            outp[own, rows, :] = total.astype(BF)
        xo_copy(way, sub, t).start()

    ST_AXES = (("y", 4), ("z", 4), ("x", 4), ("c", 2))

    def st_copy(ph, slot, k):
        axis, size = ST_AXES[ph]
        device = {axis: lax.rem(me[axis] + k, size)}
        ref = stat.at[ph, slot]
        return remote(ref, ref, st_send.at[ph, k], st_recv.at[ph, slot], device)

    def st_start(ph, total):
        axis, size = ST_AXES[ph]
        stat[ph, me[axis]] = total
        for k in range(1, size):
            st_copy(ph, me[axis], k).start()

    def st_finish(ph):
        axis, size = ST_AXES[ph]
        for k in range(1, size):
            st_copy(ph, lax.rem(me[axis] + k, size), k).wait_recv()
        total = stat[ph, 0]
        for k in range(1, size):
            total = total + stat[ph, k]
        return total

    def tile(n):
        return pl.ds(pl.multiple_of(n * TILE, TILE), TILE)

    def weights(a, n):
        return full[a, :, :, :, :, tile(n)].reshape(D, TILE)

    def fold(v):
        v = jnp.sum(v.reshape(TOK // 8, 8, TILE), axis=0)
        return v[:, :128] + v[:, 128:]

    def fisher_tile(n):
        product = jnp.dot(xf[0], weights(0, n), preferred_element_type=F32)
        value = ((product * gate[:, tile(n)].astype(F32)) ** 2).astype(BF)
        fish[:, tile(n)] = value
        gate_t[tile(n), :] = jnp.transpose(value)
        acc[0] += fold(value.astype(F32))

    def residual_tile(n):
        residual = jnp.dot(xf[1], weights(1, n), preferred_element_type=F32)
        weighted = fish[:, tile(n)].astype(F32) * residual
        wbuf[:, tile(n)] = weighted.astype(BF)
        acc[1] += fold(weighted * residual)

    def grad_tile(n):
        right = wbuf[:, tile(n)]
        for q in range(4):
            product = jnp.dot(feats_t[q], right, preferred_element_type=F32)
            grad[q, :, :, :, tile(n)] = product.astype(BF).reshape(4, 2, ROWS, TILE)

    def hidden_tile(n):
        product = jnp.dot(xf[1], weights(2, n), preferred_element_type=F32)
        wbuf[:, tile(n)] = (product * gate[:, tile(n)].astype(F32)).astype(BF)

    def out_tile(i):
        target = at("x", 3 - 2 * i + (i // 2) * 3)
        right = full[0, target].reshape(XW, FFP)
        product = lax.dot_general(wbuf[...], right, (((1,), (1,)), ((), ())), preferred_element_type=F32)
        outp[target] = product.astype(BF)

    own_cols = pl.ds(pl.multiple_of(x * XW, XW), XW)
    loads = [
        pltpu.make_async_copy(down_in, down_own, local.at[0]),
        pltpu.make_async_copy(logit_in, logit, local.at[1]),
        pltpu.make_async_copy(offset_in, offset, local.at[2]),
        pltpu.make_async_copy(step_in, step_own, local.at[3]),
        pltpu.make_async_copy(go, xf.at[0, :, own_cols], local.at[4]),
        pltpu.make_async_copy(up_in, up_own, local.at[5]),
        pltpu.make_async_copy(bi, xf.at[1, :, own_cols], local.at[6]),
        pltpu.make_async_copy(gate_in, gate_t.at[pl.ds(0, FF), :], local.at[7]),
    ]
    for load in loads:
        load.start()
    barrier = pltpu.get_barrier_semaphore()
    partners = [{axis: at(axis, k)} for axis in ("z", "y", "x") for k in (1, 2, 3)] + [other]
    for device in partners:
        pl.semaphore_signal(barrier, inc=1, device_id=device, device_id_type=MESH)
    acc[...] = jnp.zeros_like(acc)
    gate_t[FF:, :] = jnp.zeros((FFP - FF, TOK), BF)
    for a in range(3):
        full[a, z, y, c, :, FFP - 128:] = jnp.zeros((ROWS, 128), BF)
    loads[0].wait()
    full[0, z, y, c, :, :FF] = down_own[...]
    for i in (1, 2, 3):
        loads[i].wait()
    soft = jax.nn.sigmoid(logit[...])
    full[1, z, y, c, :, :FF] = (step_own[...] * (soft - offset[...].astype(F32))).astype(BF)
    loads[5].wait()
    full[2, z, y, c, :, :FF] = up_own[...]
    loads[4].wait()
    loads[6].wait()
    pl.semaphore_wait(barrier, len(partners))

    ag_start(0)
    for i in (0, 1):
        x_start(0, i)
    ag_start(1)
    for i in (0, 1):
        x_start(1, i)
    for d in (1, 2, 3):
        ag_first(0, d)
    soft = jax.nn.sigmoid(logit[...])
    centered = 2.0 * soft - 1.0
    sig_slope = soft * (1.0 - soft)
    slope[...] = step_own[...] * sig_slope
    pull[...] = REG_WEIGHT * 8.0 * centered**3 * sig_slope
    reg_sum = jnp.sum(1.0 - (centered * centered) ** 2, axis=(0, 1), keepdims=True)
    acc[2] = jnp.broadcast_to(reg_sum * (1.0 / 1024.0), (8, 128))
    loads[7].wait()


    @pl.loop(0, 3)
    def _(n):
        ag_second(0, n)
        gate[:, tile(n)] = jnp.transpose(gate_t[tile(n), :])

    for i in (0, 1):
        x_wait(0, i)
    for i in (2, 3):
        x_start(0, i)

    @pl.loop(3, 6)
    def _(n):
        ag_second(0, n)
        ag_first(1, n - 2)
        gate[:, tile(n)] = jnp.transpose(gate_t[tile(n), :])

    @pl.loop(6, 10)
    def _(n):
        ag_second(0, n)
        ag_second(1, n - 6)

        @pl.when(n == 6)
        def _():
            gate[:, tile(n)] = jnp.transpose(gate_t[tile(n), :])

    for i in (0, 1):
        x_wait(1, i)
    for i in (2, 3):
        x_start(1, i)

    @pl.loop(10, 12)
    def _(n):
        ag_second(0, n)
        ag_second(1, n - 6)

    ag_start(2)
    for i in (2, 3):
        x_wait(0, i)
    ag_finish(0)

    @pl.loop(0, NT)
    def _(n):
        @pl.when(n < 6)
        def _():
            ag_second(1, n + 6)

        @pl.when((n >= 2) & (n < 5))
        def _():
            ag_first(2, n - 1)

        fisher_tile(n)

    save_fisher = pltpu.make_async_copy(gate_t.at[pl.ds(0, FF), :], fisher_out, local.at[7])
    save_fisher.start()
    ag_second(2, 0)
    for i in (2, 3):
        x_wait(1, i)
    for q in range(4):
        feats_t[q] = jnp.transpose(xf[1, :, q * XW:(q + 1) * XW])
        if q % 2:
            ag_second(2, (q + 1) // 2)
    ag_finish(1)

    def rs_begin(s):
        pair_copy(s).wait_recv()

        @pl.loop(0, 4)
        def _(j):
            rs_step(s, 0, j)

    @pl.loop(0, NT)
    def _(n):
        residual_tile(n)
        ag_second(2, n + 3)
        grad_tile(n)
        for s in range(STREAMS):
            @pl.when(n == READY[s])
            def _():
                pair_copy(s).start()

        for s in EARLY:
            @pl.when(n == READY[s] + 1)
            def _():
                rs_begin(s)

    ag_second(2, 10)
    st_start(0, acc[...])
    for s in LATE:
        rs_begin(s)

    ag_second(2, 11)
    st_start(1, st_finish(0))
    ag_finish(2)

    @pl.loop(0, NT)
    def _(n):
        hidden_tile(n)

        @pl.when((n >= 2) & (n < 6))
        def _():
            for s in range(STREAMS):
                rs_step(s, 1, n - 2)

    st_start(2, st_finish(1))

    def rs_round(t, j):
        for s in range(STREAMS):
            rs_step(s, t, j)

    def xo_round(t, ways=(0, 1)):
        for sub in range(SUBS):
            for way in ways:
                xo_step(way, sub, t)

    @pl.loop(0, 4)
    def _(i):
        out_tile(i)

        @pl.when(i == 0)
        def _():
            xo_round(0, (0,))

        @pl.when(i == 1)
        def _():
            xo_round(0, (1,))

        @pl.when(i < 2)
        def _():
            rs_round(2, 2 * i)
            rs_round(2, 2 * i + 1)

        @pl.when(i == 2)
        def _():
            xo_round(1)
            rs_round(3, 0)

    rs_round(3, 1)
    xo_round(2)
    rs_round(3, 2)
    st_start(3, st_finish(2))
    rs_round(3, 3)
    sums = st_finish(3)
    fisher_sum, recon_sum, reg_sum = (jnp.sum(sums[i], axis=(0, 1), keepdims=True) for i in range(3))
    fisher_mean = fisher_sum / CELLS
    loss_out[...] = recon_sum / (fisher_mean * CELLS) + REG_WEIGHT * reg_sum / WEIGHT_CELLS
    grad_logit[...] = gsum[:, :FF] * (2.0 / fisher_mean) * slope[...] - pull[...]
    xo_round(3)

    for a in range(3):
        ag_drain(a)
    for t in range(2):
        for i in range(4):
            x_copy(t, i, X_MOVES[i][0]).wait_send()
    for s in range(STREAMS):
        pair_copy(s).wait_send()
        ref = ring.at[:, *part(s)]
        remote(ref, ref, rs_send.at[s], rs_recv.at[s, 0], other).wait_send()
    for way in range(2):
        for sub in range(SUBS):
            for t in range(3):
                xo_copy(way, sub, t).wait_send()
    for ph in range(4):
        for k in range(1, ST_AXES[ph][1]):
            st_copy(ph, me[ST_AXES[ph][0]], k).wait_send()
    save_fisher.wait()


def run(*operands):
    vmem, hbm = pl.BlockSpec(memory_space=pltpu.VMEM), pl.BlockSpec(memory_space=pl.ANY)
    dma = pltpu.SemaphoreType.DMA
    return pl.pallas_call(
        kernel,
        out_shape=(
            jax.ShapeDtypeStruct((TOK, XW), BF),
            jax.ShapeDtypeStruct((FF, TOK), BF),
            jax.ShapeDtypeStruct((ROWS, FF), F32),
            jax.ShapeDtypeStruct((1, 1), F32),
        ),
        in_specs=[hbm] * 8,
        out_specs=(vmem, hbm, vmem, vmem),
        scratch_shapes=[
            pltpu.VMEM((3, 4, 4, 2, ROWS, FFP), BF),
            pltpu.VMEM((2, TOK, D), BF),
            pltpu.VMEM((4, XW, TOK), BF),
            pltpu.VMEM((TOK, FFP), BF),
            pltpu.VMEM((FFP, TOK), BF),
            pltpu.VMEM((TOK, FFP), BF),
            pltpu.VMEM((TOK, FFP), BF),
            pltpu.VMEM((4, 4, 2, ROWS, FFP), BF),
            pltpu.VMEM((4, 4, ROWS, FFP), BF),
            pltpu.VMEM((15, ROWS, FFP), BF),
            pltpu.VMEM((4, TOK, XW), BF),
            pltpu.VMEM((3, TOK, XW), BF),
            pltpu.VMEM((3, 8, 128), F32),
            pltpu.VMEM((4, 4, 3, 8, 128), F32),
            pltpu.VMEM((ROWS, FF), BF),
            pltpu.VMEM((ROWS, FF), BF),
            pltpu.VMEM((1, FF), F32),
            pltpu.VMEM((ROWS, FF), F32),
            pltpu.VMEM((ROWS, FF), BF),
            pltpu.VMEM((ROWS, FF), F32),
            pltpu.VMEM((ROWS, FF), F32),
            pltpu.VMEM((ROWS, FFP), F32),
            dma((8,)),
            dma((3, STREAMS, 16)), dma((3, STREAMS)), dma((3, STREAMS, 4)), dma((3, STREAMS)),
            dma((2, 4)), dma((2, 4)),
            dma((STREAMS, 16)), dma((STREAMS,)), dma((STREAMS,)), dma((STREAMS,)),
            dma((2, SUBS, 3)), dma((2, SUBS, 3)),
            dma((4, 4)), dma((4, 4)),
        ],
        compiler_params=pltpu.CompilerParams(
            collective_id=0, has_side_effects=True, vmem_limit_bytes=67043328
        ),
    )(*operands)


def save_kernel(out_in, fisher_in, grad_in, loss_in, out, fisher, grad, loss, out_v, fisher_v, grad_v, loss_v, sems):
    third = FF // 3
    moves = []
    for q in range(3):
        rows = pl.ds(q * third, third)
        moves.append((fisher_in.at[rows, :], fisher_v.at[rows, :], fisher.at[rows, :]))
    moves += [(grad_in, grad_v, grad), (out_in, out_v, out), (loss_in, loss_v, loss)]
    reads = [pltpu.make_async_copy(src, mid, sems.at[0, i]) for i, (src, mid, _) in enumerate(moves)]
    writes = [pltpu.make_async_copy(mid, dst, sems.at[1, i]) for i, (_, mid, dst) in enumerate(moves)]
    for read in reads:
        read.start()
    for read, write in zip(reads, writes):
        read.wait()
        write.start()
    for write in writes:
        write.wait()


def save(*arrays):
    hbm = pl.BlockSpec(memory_space=pl.ANY)
    return pl.pallas_call(
        save_kernel,
        out_shape=tuple(jax.ShapeDtypeStruct(a.shape, a.dtype) for a in arrays),
        in_specs=[hbm] * 4,
        out_specs=(hbm,) * 4,
        scratch_shapes=[pltpu.VMEM(a.shape, a.dtype) for a in arrays] + [pltpu.SemaphoreType.DMA((2, 6))],
    )(*arrays)


def body(
    block_input, gate_act, grad_out, up_weight, down_weight, quant_step, round_logit, grid_offset
):
    block_output, fisher_t, grad_logit, loss = save(*run(
        block_input, gate_act.T, grad_out, up_weight, down_weight.T, quant_step[None, :], round_logit, grid_offset
    ))
    return (block_output, fisher_t.T, grad_logit, loss[0, 0])


def solution(mesh):
    torus = Mesh(mesh.devices.reshape(4, 4, 2, 4), ("z", "y", "c", "x"))
    dp = ("z", "y", "c")
    in_specs = (
        P(dp, "x"), P(dp, "x"), P(dp, "x"), P(dp, "x"), P("x", dp), P("x"), P(dp, "x"), P(dp, "x"),
    )
    out_specs = (P(dp, "x"), P(dp, "x"), P(dp, "x"), P())
    return jax.shard_map(body, mesh=torus, in_specs=in_specs, out_specs=out_specs, check_vma=False)
```

time: 161 us -> 143 us (0.89)
  local copies, waits for them, and re-layouts: 8.58 us -> 1.3 us
  other arithmetic: 4.76 us -> 0 us
  between operations: 5.18 us -> 0.64 us
    unnamed x17 -> x0, local copies, waits for them, and re-layouts: 5.72 us -> none
    pallas_call x1, Pallas kernels: 141 us -> 138 us  [run(): pl.pallas_call(kernel, out_shape=(jax.ShapeDtypeStruct((TOK, XW), BF), ja...]
    pallas_call x0 -> x1, Pallas kernels: none -> 3.21 us  [save(): pl.pallas_call(save_kernel, out_shape=tuple((jax.ShapeDtypeStruct(a.shape...]
    reduce_sum x2 -> x0, other arithmetic: 2.63 us -> none  [the longest x1 2.03 us: body(): reg_local = jnp.sum(1.0 - (centered * centered) ** 2)]
where the time goes in v2:
time: 143 us
  Pallas kernels  141 us (99%)
    pallas_call x1, Pallas kernels, run(): pl.pallas_call(kernel, out_shape=(jax.ShapeDtypeStruct((TOK, XW), BF), ja...  138 us
    pallas_call x1, Pallas kernels, save(): pl.pallas_call(save_kernel, out_shape=tuple((jax.ShapeDtypeStruct(a.shape...  3.21 us

profile of v2, /device:TPU:0, one launch (start us, length us, event | category | flops | bytes accessed | tf_op | source)
XLA Modules:
  0.0 142.7 jit_solution(13069617080538286091)
XLA Ops:
  0.6 1.3 broadcast_in_dim.3.step_in
  1.9 137.6 %shard_map.111 = (bf16[384,640]{1,0:T(8,128)(2,1)}, bf16[1728,384]{1,0:T(8,128)(2,1)}, f32[80,1728]{1,0:T(8,128)}, f32[1,1]{1,0:T(1,128)}) custom-call(bf16[384,640]{1,0:T(8,128)(2,1)} %bi.1, bf16[1728,384]{1,0:T(8,128)(2,1)} %bitcast.4, bf16[384,640]{1,0:T(8,128)(2,1)} %go.1, bf16[80,1728]{1,0:T(8,128)(2,1)} %up_in.1, bf16[80,1728]{1,0:T(8,128)(2,1)} %bitcast.5, ...), custom_call_target="tpu_custom_call" | custom-call | tf_op jit(solution)/shard_map/pallas_call | solution.py:499
  139.5 3.2 %shard_map.112 = (bf16[384,640]{1,0:T(8,128)(2,1)}, bf16[1728,384]{1,0:T(8,128)(2,1)}, f32[80,1728]{1,0:T(8,128)}, f32[1,1]{1,0:T(1,128)}) custom-call(bf16[384,640]{1,0:T(8,128)(2,1)} %get-tuple-element.12.out_in, bf16[1728,384]{1,0:T(8,128)(2,1)} %get-tuple-element.13.fisher_in, f32[80,1728]{1,0:T(8,128)} %get-tuple-element.14.grad_in, ...), custom_call_target="tpu_custom_call" | custom-call | tf_op jit(solution)/shard_map/pallas_call | solution.py:565

commit v3 on v2

v3 whole, which is shorter than its diff:
```python
import jax
import jax.numpy as jnp
from jax import lax
from jax.experimental import pallas as pl
from jax.experimental.pallas import tpu as pltpu
from jax.sharding import Mesh
from jax.sharding import PartitionSpec as P

D = 2560
FFW = 6912
TOK = 384
FF = 1728
FFP = 1792
ROWS = 80
XW = 640
TILE = 256
NT = FFP // TILE
REG_WEIGHT = 0.5
CELLS = 12288 * FFW
WEIGHT_CELLS = D * FFW
BF = jnp.bfloat16
F32 = jnp.float32
MESH = pl.DeviceIdType.MESH

GATHER = (("y", "z"), ("z", "y"))
REDUCE = (("z", "y"), ("y", "z"))
SPAN = FFP // 2
READY = (3, 6)
PLACES = (0, -1, 1, 2)
TURNS = (2, 1, -1, 0)
ALL = (0, ROWS)
HALVES = ((0, 48), (48, 32))
SUBS = 3
SUB_ROWS = TOK // SUBS


def kernel(
    bi, gate_in, go, up_in, down_in, step_in, logit_in, offset_in,
    block_out, fisher_out, grad_logit, loss_out,
    full, xf, feats_t, gate, gate_t, fish, wbuf, grad, pair, ring, outp, outr, acc, stat,
    weight_own, step_own, logit, offset, slope, pull,
    local, ag_recv, ag_send, pr_recv, pr_send, x_recv, x_send,
    rs_recv, rs_send, pe_recv, pe_send, xo_recv, xo_send, st_recv, st_send,
):
    me = {name: lax.axis_index(name) for name in ("z", "y", "c", "x")}
    z, y, c, x = me["z"], me["y"], me["c"], me["x"]
    other = {"c": 1 - c}

    def at(axis, k):
        return lax.rem(me[axis] + (k + 4), 4)

    def step_to(axis, sign):
        return {axis: at(axis, sign)}

    def remote(src, dst, send, recv, device):
        return pltpu.make_async_remote_copy(
            src_ref=src, dst_ref=dst, send_sem=send, recv_sem=recv, device_id=device, device_id_type=MESH
        )

    def piece(a, s, d, e, rows):
        first, second = GATHER[s]
        co = {first: at(first, d), second: at(second, e)}
        return full.at[a, co["z"], co["y"], c, pl.ds(*rows), pl.ds(s * SPAN, SPAN)]

    def move(a, s, d, e, rows, axis, sign, slot):
        ref = piece(a, s, d, e, rows)
        remote(ref, ref, ag_send.at[a, s], ag_recv.at[a, s, slot], step_to(axis, sign)).start()

    def wait_piece(a, s, d, e, rows, slot):
        ref = piece(a, s, d, e, rows)
        remote(ref, ref, ag_send.at[a, s], ag_recv.at[a, s, slot], other).wait_recv()

    def along_second(a, s, i):
        for sign, slot in ((1, 0), (-1, 1)):
            move(a, s, PLACES[i], 0, ALL, GATHER[s][1], sign, 4 + 4 * i + slot)

    def forward_second(a, i):
        for s in range(2):
            d, h = PLACES[i], (s + i) % 2
            wait_piece(a, s, d, -1, ALL, 4 + 4 * i)
            move(a, s, d, -1, HALVES[h], GATHER[s][1], 1, 6 + 4 * i)
            wait_piece(a, s, d, 1, ALL, 5 + 4 * i)
            move(a, s, d, 1, HALVES[1 - h], GATHER[s][1], -1, 7 + 4 * i)

    def bundle(a, s, e, parity):
        second = GATHER[s][1]
        cols = pl.ds(s * SPAN, SPAN)
        if second == "z":
            return full.at[a, at("z", e), :, parity, :, cols]
        return full.at[a, :, at("y", e), parity, :, cols]

    def send_pair(a, i):
        for s in range(2):
            ref = bundle(a, s, PLACES[i], c)
            remote(ref, ref, pr_send.at[a, s], pr_recv.at[a, s, i], other).start()

    def ag_start(a):
        for s in range(2):
            for sign, slot in ((1, 0), (-1, 1)):
                move(a, s, 0, 0, ALL, GATHER[s][0], sign, slot)
        for s in range(2):
            along_second(a, s, 0)

    def ag_event(a, k):
        if k == 0:
            for s in range(2):
                first = GATHER[s][0]
                wait_piece(a, s, -1, 0, ALL, 0)
                move(a, s, -1, 0, HALVES[s], first, 1, 2)
                wait_piece(a, s, 1, 0, ALL, 1)
                move(a, s, 1, 0, HALVES[1 - s], first, -1, 3)
            for i in (1, 2):
                for s in range(2):
                    along_second(a, s, i)
        elif k == 1:
            forward_second(a, 0)
        elif k == 2:
            for s in range(2):
                wait_piece(a, s, 2, 0, HALVES[s], 2)
                wait_piece(a, s, 2, 0, HALVES[1 - s], 3)
                along_second(a, s, 3)
            send_pair(a, 0)
        elif k < 6:
            forward_second(a, k - 2)
            if k == 5:
                send_pair(a, 1)
                send_pair(a, 2)
        else:
            for i in range(4):
                for s in range(2):
                    h = (s + i) % 2
                    wait_piece(a, s, PLACES[i], 2, HALVES[h], 6 + 4 * i)
                    wait_piece(a, s, PLACES[i], 2, HALVES[1 - h], 7 + 4 * i)
            send_pair(a, 3)

    def ag_finish(a):
        for s in range(2):
            for i in range(4):
                ref = bundle(a, s, PLACES[i], 1 - c)
                remote(ref, ref, pr_send.at[a, s], pr_recv.at[a, s, i], other).wait_recv()

    def ag_drain(a):
        for s in range(2):
            ref = ring.at[:, :, pl.ds(s * SPAN, SPAN)]
            remote(ref, ref, ag_send.at[a, s], ag_recv.at[a, s, 0], other).wait_send()
            ref = full.at[a, :, :, c, :, pl.ds(s * SPAN, SPAN)]
            remote(ref, ref, pr_send.at[a, s], pr_recv.at[a, s, 0], other).wait_send()

    def x_block(t, k, lo, count):
        return xf.at[t, pl.ds(lo, count), pl.ds(pl.multiple_of(at("x", k) * XW, XW), XW)]

    X_MOVES = ((0, 1, 0, TOK, -1), (0, -1, 0, TOK, 1), (-1, 1, 0, TOK // 2, 2), (1, -1, TOK // 2, TOK // 2, 2))

    def x_copy(t, i, k):
        src, sign, lo, count, got = X_MOVES[i]
        ref = x_block(t, k, lo, count)
        return remote(ref, ref, x_send.at[t, i], x_recv.at[t, i], step_to("x", sign))

    def x_start(t, i):
        x_copy(t, i, X_MOVES[i][0]).start()

    def x_wait(t, i):
        x_copy(t, i, X_MOVES[i][4]).wait_recv()

    def pair_copy(s):
        cols = pl.ds(s * SPAN, SPAN)
        return remote(grad.at[:, :, 1 - c, :, cols], pair.at[:, :, :, cols], pe_send.at[s], pe_recv.at[s], other)

    class Block:
        def __init__(self, s, d, e):
            first, second = REDUCE[s]
            self.s = s
            self.co = {first: at(first, d), second: at(second, e)}

        def ref(self, rows):
            return grad.at[self.co["z"], self.co["y"], c, pl.ds(*rows), pl.ds(self.s * SPAN, SPAN)]

        def sum(self, rows, *slots):
            cols = pl.ds(self.s * SPAN, SPAN)
            total = self.ref(rows)[...].astype(F32)
            total = total + pair[self.co["z"], self.co["y"], pl.ds(*rows), cols].astype(F32)
            for slot in slots:
                total = total + ring[slot, pl.ds(*rows), cols].astype(F32)
            return total

        def copy(self, rows, slot, sem, axis, sign):
            dst = ring.at[slot, pl.ds(*rows), pl.ds(self.s * SPAN, SPAN)]
            device = other if axis is None else step_to(axis, sign)
            return remote(self.ref(rows), dst, rs_send.at[self.s], rs_recv.at[self.s, sem], device)

        def send(self, rows, slot, sem, axis, sign):
            self.copy(rows, slot, sem, axis, sign).start()

        def wait(self, rows, slot, sem):
            self.copy(rows, slot, sem, None, 0).wait_recv()

    def rs_far(s, j):
        first, h = REDUCE[s][0], (s + j) % 2
        block = Block(s, 2, TURNS[j])
        block.ref(ALL)[...] = block.sum(ALL).astype(BF)
        block.send(HALVES[h], j, 4 * j, first, 1)
        block.send(HALVES[1 - h], j, 4 * j + 1, first, -1)

    def rs_near(s, j):
        first = REDUCE[s][0]
        for sign, side in ((1, 0), (-1, 1)):
            h = (s + j + side) % 2
            block = Block(s, sign, TURNS[j])
            block.wait(HALVES[h], j, 4 * j + side)
            rest = block.sum(HALVES[1 - h]).astype(BF)
            block.ref(HALVES[1 - h])[...] = rest
            block.ref(HALVES[h])[...] = block.sum(HALVES[h], j).astype(BF)
            block.send(ALL, 4 + 4 * side + j, 4 * j + 2 + side, first, sign)

    def rs_own(s, j):
        second, h = REDUCE[s][1], s
        block = Block(s, 0, TURNS[j])
        block.wait(ALL, 4 + j, 4 * j + 2)
        block.wait(ALL, 8 + j, 4 * j + 3)
        if j == 0:
            block.ref(ALL)[...] = block.sum(ALL, 4 + j, 8 + j).astype(BF)
            block.send(HALVES[h], 12, 16, second, 1)
            block.send(HALVES[1 - h], 12, 17, second, -1)
        elif j < 3:
            side = j - 1
            h = (h + side) % 2
            block.wait(HALVES[h], 12, 16 + side)
            rest = block.sum(HALVES[1 - h], 4 + j, 8 + j).astype(BF)
            block.ref(HALVES[1 - h])[...] = rest
            block.ref(HALVES[h])[...] = block.sum(HALVES[h], 4 + j, 8 + j, 12).astype(BF)
            block.send(ALL, 13 + side, 18 + side, second, 1 - 2 * side)
        else:
            block.wait(ALL, 13, 18)
            block.wait(ALL, 14, 19)
            total = block.sum(ALL, 4 + j, 8 + j, 13, 14)
            if s == 0:
                logit[:, :SPAN] = total
            else:
                logit[:, SPAN:] = total[:, :FF - SPAN]

    def xo_rows(sub, half=None):
        if half is None:
            return pl.ds(sub * SUB_ROWS, SUB_ROWS)
        return pl.ds(sub * SUB_ROWS + half * (SUB_ROWS // 2), SUB_ROWS // 2)

    def xo_copy(sub, k):
        side, far = k % 2, k < 2
        rows = xo_rows(sub, side if far else None)
        target = at("x", 2 if far else 1 - 2 * side)
        return remote(
            outp.at[target, rows, :], outr.at[0 if far else 1 + side, rows, :],
            xo_send.at[sub, k], xo_recv.at[sub, k], step_to("x", 1 - 2 * side),
        )

    def xo_far(sub):
        for k in (0, 1):
            xo_copy(sub, k).start()

    def xo_near(sub, side):
        target, rows = at("x", 1 - 2 * side), xo_rows(sub, side)
        xo_copy(sub, side).wait_recv()
        total = outp[target, rows, :].astype(F32) + outr[0, rows, :].astype(F32)
        outp[target, rows, :] = total.astype(BF)
        xo_copy(sub, 2 + side).start()

    def xo_own(sub):
        rows = xo_rows(sub)
        for k in (2, 3):
            xo_copy(sub, k).wait_recv()
        total = outp[x, rows, :].astype(F32) + outr[1, rows, :].astype(F32) + outr[2, rows, :].astype(F32)
        block_out[rows, :] = total.astype(BF)

    def xo_all(step, *args):
        for sub in range(SUBS):
            step(sub, *args)

    ST_AXES = (("y", 4), ("z", 4), ("x", 4), ("c", 2))

    def st_copy(ph, slot, k):
        axis, size = ST_AXES[ph]
        device = {axis: lax.rem(me[axis] + k, size)}
        ref = stat.at[ph, slot]
        return remote(ref, ref, st_send.at[ph, k], st_recv.at[ph, slot], device)

    def st_start(ph, total):
        axis, size = ST_AXES[ph]
        stat[ph, me[axis]] = total
        for k in range(1, size):
            st_copy(ph, me[axis], k).start()

    def st_finish(ph):
        axis, size = ST_AXES[ph]
        for k in range(1, size):
            st_copy(ph, lax.rem(me[axis] + k, size), k).wait_recv()
        total = stat[ph, 0]
        for k in range(1, size):
            total = total + stat[ph, k]
        return total

    def tile(n):
        return pl.ds(pl.multiple_of(n * TILE, TILE), TILE)

    def weights(a, n):
        return full[a, :, :, :, :, tile(n)].reshape(D, TILE)

    def fold(v):
        v = jnp.sum(v.reshape(TOK // 8, 8, TILE), axis=0)
        return v[:, :128] + v[:, 128:]

    def fisher_tile(n):
        product = jnp.dot(xf[0], weights(0, n), preferred_element_type=F32)
        value = ((product * gate[:, tile(n)].astype(F32)) ** 2).astype(BF)
        fish[:, tile(n)] = value
        gate_t[tile(n), :] = jnp.transpose(value)
        acc[0] += fold(value.astype(F32))

    def residual_tile(n):
        residual = jnp.dot(xf[1], weights(1, n), preferred_element_type=F32)
        weighted = fish[:, tile(n)].astype(F32) * residual
        wbuf[:, tile(n)] = weighted.astype(BF)
        acc[1] += fold(weighted * residual)

    def grad_tile(n):
        right = wbuf[:, tile(n)]
        for q in range(4):
            product = jnp.dot(feats_t[q], right, preferred_element_type=F32)
            grad[q, :, :, :, tile(n)] = product.astype(BF).reshape(4, 2, ROWS, TILE)

    def hidden_tile(n):
        product = jnp.dot(xf[1], weights(2, n), preferred_element_type=F32)
        wbuf[:, tile(n)] = (product * gate[:, tile(n)].astype(F32)).astype(BF)

    def out_tile(i):
        target = at("x", jnp.where(i == 2, 3, jnp.where(i == 3, 0, 2 - i)))
        right = full[0, target].reshape(XW, FFP)
        product = lax.dot_general(wbuf[...], right, (((1,), (1,)), ((), ())), preferred_element_type=F32)
        outp[target] = product.astype(BF)

    own_cols = pl.ds(pl.multiple_of(x * XW, XW), XW)
    loads = [
        pltpu.make_async_copy(down_in, weight_own, local.at[0]),
        pltpu.make_async_copy(logit_in, logit, local.at[1]),
        pltpu.make_async_copy(offset_in, offset, local.at[2]),
        pltpu.make_async_copy(step_in, step_own, local.at[3]),
        pltpu.make_async_copy(go, xf.at[0, :, own_cols], local.at[4]),
        pltpu.make_async_copy(up_in, weight_own, local.at[5]),
        pltpu.make_async_copy(bi, xf.at[1, :, own_cols], local.at[6]),
        pltpu.make_async_copy(gate_in, gate_t.at[pl.ds(0, FF), :], local.at[7]),
    ]
    for i, load in enumerate(loads):
        if i != 5:
            load.start()
    barrier = pltpu.get_barrier_semaphore()
    partners = [{axis: at(axis, k)} for axis in ("z", "y", "x") for k in (1, 2, 3)] + [other]
    for device in partners:
        pl.semaphore_signal(barrier, inc=1, device_id=device, device_id_type=MESH)
    acc[...] = jnp.zeros_like(acc)
    gate_t[FF:, :] = jnp.zeros((FFP - FF, TOK), BF)
    for a in range(3):
        full[a, z, y, c, :, FFP - 128:] = jnp.zeros((ROWS, 128), BF)
    loads[0].wait()
    full[0, z, y, c, :, :FF] = weight_own[...]
    for i in (1, 2, 3):
        loads[i].wait()
    soft = jax.nn.sigmoid(logit[...])
    full[1, z, y, c, :, :FF] = (step_own[...] * (soft - offset[...].astype(F32))).astype(BF)
    loads[4].wait()
    loads[6].wait()
    pl.semaphore_wait(barrier, len(partners))

    def on(index, value, *calls):
        @pl.when(index == value)
        def _():
            for call, *args in calls:
                call(*args)

    ag_start(0)
    for i in (0, 1):
        x_start(0, i)
    soft = jax.nn.sigmoid(logit[...])
    centered = 2.0 * soft - 1.0
    sig_slope = soft * (1.0 - soft)
    slope[...] = step_own[...] * sig_slope
    pull[...] = REG_WEIGHT * 8.0 * centered**3 * sig_slope
    reg_sum = jnp.sum(1.0 - (centered * centered) ** 2, axis=(0, 1), keepdims=True)
    acc[2] = jnp.broadcast_to(reg_sum * (1.0 / 1024.0), (8, 128))
    loads[7].wait()
    loads[5].start()
    ag_event(0, 0)
    ag_event(0, 1)

    @pl.loop(0, NT)
    def _(n):
        gate[:, tile(n)] = jnp.transpose(gate_t[tile(n), :])
        on(n, 1, (ag_event, 0, 2))
        on(n, 3, (ag_event, 0, 3))
        on(n, 6, (ag_event, 0, 4))

    for i in (0, 1):
        x_wait(0, i)
    for i in (2, 3):
        x_start(0, i)
    for i in (0, 1):
        x_start(1, i)
    loads[5].wait()
    full[2, z, y, c, :, :FF] = weight_own[...]
    ag_event(0, 5)
    ag_start(1)
    ag_event(0, 6)
    for i in (2, 3):
        x_wait(0, i)
    ag_finish(0)

    @pl.loop(0, NT)
    def _(n):
        for k in range(5):
            on(n, k + 1, (ag_event, 1, k))
        fisher_tile(n)

    save_fisher = pltpu.make_async_copy(gate_t.at[pl.ds(0, FF), :], fisher_out, local.at[7])
    save_fisher.start()
    for i in (0, 1):
        x_wait(1, i)
    for i in (2, 3):
        x_start(1, i)
    ag_event(1, 5)
    ag_start(2)
    ag_event(1, 6)
    for i in (2, 3):
        x_wait(1, i)
    for q in range(4):
        feats_t[q] = jnp.transpose(xf[1, :, q * XW:(q + 1) * XW])
    ag_finish(1)

    @pl.loop(0, NT)
    def _(n):
        residual_tile(n)
        for k in range(6):
            on(n, k, (ag_event, 2, k))
        grad_tile(n)
        on(n, READY[0], (lambda: pair_copy(0).start(),))
        on(n, READY[1], (lambda: pair_copy(1).start(),))
        on(n, 5, (lambda: pair_copy(0).wait_recv(),), (rs_far, 0, 0), (rs_far, 0, 1))
        on(n, 6, (rs_near, 0, 0), (rs_far, 0, 2), (rs_near, 0, 1), (rs_far, 0, 3))

    st_start(0, acc[...])
    ag_event(2, 6)
    rs_near(0, 2)
    pair_copy(1).wait_recv()
    rs_far(1, 0)
    rs_far(1, 1)
    rs_near(0, 3)
    ag_finish(2)
    st_start(1, st_finish(0))

    @pl.loop(0, NT)
    def _(n):
        hidden_tile(n)
        on(n, 1, (rs_own, 0, 0))
        on(n, 3, (rs_near, 1, 0), (rs_far, 1, 2))
        on(n, 5, (rs_near, 1, 1), (rs_far, 1, 3))
        on(n, 6, (rs_own, 0, 1), (rs_own, 0, 2))

    st_start(2, st_finish(1))

    @pl.loop(0, 4)
    def _(i):
        out_tile(i)
        on(i, 0, (xo_all, xo_far), (rs_near, 1, 2), (rs_own, 1, 0))
        on(i, 1, (rs_near, 1, 3), (rs_own, 0, 3))
        on(i, 2, (xo_all, xo_near, 0), (xo_all, xo_near, 1), (rs_own, 1, 1))
        on(i, 3, (rs_own, 1, 2))

    st_start(3, st_finish(2))
    rs_own(1, 3)
    sums = st_finish(3)
    fisher_sum, recon_sum, reg_sum = (jnp.sum(sums[i], axis=(0, 1), keepdims=True) for i in range(3))
    fisher_mean = fisher_sum / CELLS
    loss_out[...] = recon_sum / (fisher_mean * CELLS) + REG_WEIGHT * reg_sum / WEIGHT_CELLS
    grad_logit[...] = logit[...] * (2.0 / fisher_mean) * slope[...] - pull[...]
    xo_all(xo_own)

    for a in range(3):
        ag_drain(a)
    for t in range(2):
        for i in range(4):
            x_copy(t, i, X_MOVES[i][0]).wait_send()
    for s in range(2):
        pair_copy(s).wait_send()
        ref = ring.at[:, :, pl.ds(s * SPAN, SPAN)]
        remote(ref, ref, rs_send.at[s], rs_recv.at[s, 0], other).wait_send()
    for sub in range(SUBS):
        for k in range(4):
            xo_copy(sub, k).wait_send()
    for ph in range(4):
        for k in range(1, ST_AXES[ph][1]):
            st_copy(ph, me[ST_AXES[ph][0]], k).wait_send()
    save_fisher.wait()


def run(*operands):
    vmem, hbm = pl.BlockSpec(memory_space=pltpu.VMEM), pl.BlockSpec(memory_space=pl.ANY)
    dma = pltpu.SemaphoreType.DMA
    return pl.pallas_call(
        kernel,
        out_shape=(
            jax.ShapeDtypeStruct((TOK, XW), BF),
            jax.ShapeDtypeStruct((FF, TOK), BF),
            jax.ShapeDtypeStruct((ROWS, FF), F32),
            jax.ShapeDtypeStruct((1, 1), F32),
        ),
        in_specs=[hbm] * 8,
        out_specs=(vmem, hbm, vmem, vmem),
        scratch_shapes=[
            pltpu.VMEM((3, 4, 4, 2, ROWS, FFP), BF),
            pltpu.VMEM((2, TOK, D), BF),
            pltpu.VMEM((4, XW, TOK), BF),
            pltpu.VMEM((TOK, FFP), BF),
            pltpu.VMEM((FFP, TOK), BF),
            pltpu.VMEM((TOK, FFP), BF),
            pltpu.VMEM((TOK, FFP), BF),
            pltpu.VMEM((4, 4, 2, ROWS, FFP), BF),
            pltpu.VMEM((4, 4, ROWS, FFP), BF),
            pltpu.VMEM((15, ROWS, FFP), BF),
            pltpu.VMEM((4, TOK, XW), BF),
            pltpu.VMEM((3, TOK, XW), BF),
            pltpu.VMEM((3, 8, 128), F32),
            pltpu.VMEM((4, 4, 3, 8, 128), F32),
            pltpu.VMEM((ROWS, FF), BF),
            pltpu.VMEM((1, FF), F32),
            pltpu.VMEM((ROWS, FF), F32),
            pltpu.VMEM((ROWS, FF), BF),
            pltpu.VMEM((ROWS, FF), F32),
            pltpu.VMEM((ROWS, FF), F32),
            dma((8,)),
            dma((3, 2, 20)), dma((3, 2)), dma((3, 2, 4)), dma((3, 2)),
            dma((2, 4)), dma((2, 4)),
            dma((2, 20)), dma((2,)), dma((2,)), dma((2,)),
            dma((SUBS, 4)), dma((SUBS, 4)),
            dma((4, 4)), dma((4, 4)),
        ],
        compiler_params=pltpu.CompilerParams(
            collective_id=0, has_side_effects=True, vmem_limit_bytes=67043328
        ),
    )(*operands)


def save_kernel(out_in, fisher_in, grad_in, loss_in, out, fisher, grad, loss, out_v, fisher_v, grad_v, loss_v, sems):
    third = FF // 3
    moves = []
    for q in range(3):
        rows = pl.ds(q * third, third)
        moves.append((fisher_in.at[rows, :], fisher_v.at[rows, :], fisher.at[rows, :]))
    moves += [(grad_in, grad_v, grad), (out_in, out_v, out), (loss_in, loss_v, loss)]
    reads = [pltpu.make_async_copy(src, mid, sems.at[0, i]) for i, (src, mid, _) in enumerate(moves)]
    writes = [pltpu.make_async_copy(mid, dst, sems.at[1, i]) for i, (_, mid, dst) in enumerate(moves)]
    for read in reads:
        read.start()
    for read, write in zip(reads, writes):
        read.wait()
        write.start()
    for write in writes:
        write.wait()


def save(*arrays):
    hbm = pl.BlockSpec(memory_space=pl.ANY)
    return pl.pallas_call(
        save_kernel,
        out_shape=tuple(jax.ShapeDtypeStruct(a.shape, a.dtype) for a in arrays),
        in_specs=[hbm] * 4,
        out_specs=(hbm,) * 4,
        scratch_shapes=[pltpu.VMEM(a.shape, a.dtype) for a in arrays] + [pltpu.SemaphoreType.DMA((2, 6))],
    )(*arrays)


def body(
    block_input, gate_act, grad_out, up_weight, down_weight, quant_step, round_logit, grid_offset
):
    block_output, fisher_t, grad_logit, loss = save(*run(
        block_input, gate_act.T, grad_out, up_weight, down_weight.T, quant_step[None, :], round_logit, grid_offset
    ))
    return (block_output, fisher_t.T, grad_logit, loss[0, 0])


def solution(mesh):
    torus = Mesh(mesh.devices.reshape(4, 4, 2, 4), ("z", "y", "c", "x"))
    dp = ("z", "y", "c")
    in_specs = (
        P(dp, "x"), P(dp, "x"), P(dp, "x"), P(dp, "x"), P("x", dp), P("x"), P(dp, "x"), P(dp, "x"),
    )
    out_specs = (P(dp, "x"), P(dp, "x"), P(dp, "x"), P())
    return jax.shard_map(body, mesh=torus, in_specs=in_specs, out_specs=out_specs, check_vma=False)
```

time: 143 us -> 133 us (0.930)
  Pallas kernels: 141 us -> 131 us
    pallas_call x1, Pallas kernels: 138 us -> 128 us  [run(): pl.pallas_call(kernel, out_shape=(jax.ShapeDtypeStruct((TOK, XW), BF), ja...]
where the time goes in v3:
time: 133 us
  Pallas kernels  131 us (98%)
    pallas_call x1, Pallas kernels, run(): pl.pallas_call(kernel, out_shape=(jax.ShapeDtypeStruct((TOK, XW), BF), ja...  128 us
    pallas_call x1, Pallas kernels, save(): pl.pallas_call(save_kernel, out_shape=tuple((jax.ShapeDtypeStruct(a.shape...  3.21 us

profile of v3, /device:TPU:0, one launch (start us, length us, event | category | flops | bytes accessed | tf_op | source)
XLA Modules:
  0.0 133.1 jit_solution(16037297981048739080)
XLA Ops:
  0.6 1.3 broadcast_in_dim.3.step_in
  1.9 128.0 %shard_map.111 = (bf16[384,640]{1,0:T(8,128)(2,1)}, bf16[1728,384]{1,0:T(8,128)(2,1)}, f32[80,1728]{1,0:T(8,128)}, f32[1,1]{1,0:T(1,128)}) custom-call(bf16[384,640]{1,0:T(8,128)(2,1)} %bi.1, bf16[1728,384]{1,0:T(8,128)(2,1)} %bitcast.4, bf16[384,640]{1,0:T(8,128)(2,1)} %go.1, bf16[80,1728]{1,0:T(8,128)(2,1)} %up_in.1, bf16[80,1728]{1,0:T(8,128)(2,1)} %bitcast.5, ...), custom_call_target="tpu_custom_call" | custom-call | tf_op jit(solution)/shard_map/pallas_call | solution.py:504
  129.9 3.2 %shard_map.112 = (bf16[384,640]{1,0:T(8,128)(2,1)}, bf16[1728,384]{1,0:T(8,128)(2,1)}, f32[80,1728]{1,0:T(8,128)}, f32[1,1]{1,0:T(1,128)}) custom-call(bf16[384,640]{1,0:T(8,128)(2,1)} %get-tuple-element.12.out_in, bf16[1728,384]{1,0:T(8,128)(2,1)} %get-tuple-element.13.fisher_in, f32[80,1728]{1,0:T(8,128)} %get-tuple-element.14.grad_in, ...), custom_call_target="tpu_custom_call" | custom-call | tf_op jit(solution)/shard_map/pallas_call | solution.py:568

commit v4 on v3

--- a/solution.py
+++ b/solution.py
@@ -415,21 +415,18 @@
     def _(n):
         for k in range(5):
             on(n, k + 1, (ag_event, 1, k))
+        on(n, 4, (x_wait, 1, 0), (x_wait, 1, 1), (x_start, 1, 2), (x_start, 1, 3))
         fisher_tile(n)
 
     save_fisher = pltpu.make_async_copy(gate_t.at[pl.ds(0, FF), :], fisher_out, local.at[7])
     save_fisher.start()
-    for i in (0, 1):
-        x_wait(1, i)
-    for i in (2, 3):
-        x_start(1, i)
     ag_event(1, 5)
     ag_start(2)
-    ag_event(1, 6)
     for i in (2, 3):
         x_wait(1, i)
     for q in range(4):
         feats_t[q] = jnp.transpose(xf[1, :, q * XW:(q + 1) * XW])
+    ag_event(1, 6)
     ag_finish(1)
 
     @pl.loop(0, NT)
@@ -440,38 +437,36 @@
         grad_tile(n)
         on(n, READY[0], (lambda: pair_copy(0).start(),))
         on(n, READY[1], (lambda: pair_copy(1).start(),))
-        on(n, 5, (lambda: pair_copy(0).wait_recv(),), (rs_far, 0, 0), (rs_far, 0, 1))
-        on(n, 6, (rs_near, 0, 0), (rs_far, 0, 2), (rs_near, 0, 1), (rs_far, 0, 3))
+        on(n, 5, (lambda: pair_copy(0).wait_recv(),), *((rs_far, 0, j) for j in range(4)))
 
     st_start(0, acc[...])
     ag_event(2, 6)
-    rs_near(0, 2)
-    pair_copy(1).wait_recv()
-    rs_far(1, 0)
-    rs_far(1, 1)
-    rs_near(0, 3)
     ag_finish(2)
-    st_start(1, st_finish(0))
 
     @pl.loop(0, NT)
     def _(n):
         hidden_tile(n)
-        on(n, 1, (rs_own, 0, 0))
-        on(n, 3, (rs_near, 1, 0), (rs_far, 1, 2))
-        on(n, 5, (rs_near, 1, 1), (rs_far, 1, 3))
-        on(n, 6, (rs_own, 0, 1), (rs_own, 0, 2))
+        on(n, 0, (rs_near, 0, 0))
+        on(
+            n, 1, (rs_near, 0, 1), (lambda: pair_copy(1).wait_recv(),), (rs_far, 1, 0), (rs_far, 1, 1),
+            (rs_near, 0, 2), (rs_far, 1, 2), (rs_far, 1, 3),
+        )
+        on(n, 2, (rs_near, 0, 3))
+        on(n, 3, (lambda: st_start(1, st_finish(0)),))
+        on(n, 4, (rs_own, 0, 0), (rs_near, 1, 0), (rs_near, 1, 1))
+        on(n, 6, (rs_near, 1, 2))
 
     st_start(2, st_finish(1))
 
     @pl.loop(0, 4)
     def _(i):
         out_tile(i)
-        on(i, 0, (xo_all, xo_far), (rs_near, 1, 2), (rs_own, 1, 0))
-        on(i, 1, (rs_near, 1, 3), (rs_own, 0, 3))
-        on(i, 2, (xo_all, xo_near, 0), (xo_all, xo_near, 1), (rs_own, 1, 1))
-        on(i, 3, (rs_own, 1, 2))
-
-    st_start(3, st_finish(2))
+        on(i, 0, (xo_all, xo_far), (rs_own, 0, 1), (rs_own, 0, 2), (rs_near, 1, 3))
+        on(i, 1, (rs_own, 1, 0), (lambda: st_start(3, st_finish(2)),))
+        on(i, 2, (xo_all, xo_near, 0), (xo_all, xo_near, 1))
+        on(i, 3, (rs_own, 1, 1), (rs_own, 1, 2))
+
+    rs_own(0, 3)
     rs_own(1, 3)
     sums = st_finish(3)
     fisher_sum, recon_sum, reg_sum = (jnp.sum(sums[i], axis=(0, 1), keepdims=True) for i in range(3))

time: 133 us -> 131 us (0.985)
  Pallas kernels: 131 us -> 128 us
    pallas_call x1, Pallas kernels: 128 us -> 125 us  [run(): pl.pallas_call(kernel, out_shape=(jax.ShapeDtypeStruct((TOK, XW), BF), ja...]
where the time goes in v4:
time: 131 us; the launch traced here: 130 us
  Pallas kernels  128 us (98%)
    pallas_call x1, Pallas kernels, run(): pl.pallas_call(kernel, out_shape=(jax.ShapeDtypeStruct((TOK, XW), BF), ja...  125 us
    pallas_call x1, Pallas kernels, save(): pl.pallas_call(save_kernel, out_shape=tuple((jax.ShapeDtypeStruct(a.shape...  3.21 us

profile of v4, /device:TPU:0, one launch (start us, length us, event | category | flops | bytes accessed | tf_op | source)
XLA Modules:
  0.0 130.4 jit_solution(11321721061539683319)
XLA Ops:
  0.6 1.3 broadcast_in_dim.3.step_in
  1.9 125.2 %shard_map.111 = (bf16[384,640]{1,0:T(8,128)(2,1)}, bf16[1728,384]{1,0:T(8,128)(2,1)}, f32[80,1728]{1,0:T(8,128)}, f32[1,1]{1,0:T(1,128)}) custom-call(bf16[384,640]{1,0:T(8,128)(2,1)} %bi.1, bf16[1728,384]{1,0:T(8,128)(2,1)} %bitcast.4, bf16[384,640]{1,0:T(8,128)(2,1)} %go.1, bf16[80,1728]{1,0:T(8,128)(2,1)} %up_in.1, bf16[80,1728]{1,0:T(8,128)(2,1)} %bitcast.5, ...), custom_call_target="tpu_custom_call" | custom-call | tf_op jit(solution)/shard_map/pallas_call | solution.py:499
  127.2 3.2 %shard_map.112 = (bf16[384,640]{1,0:T(8,128)(2,1)}, bf16[1728,384]{1,0:T(8,128)(2,1)}, f32[80,1728]{1,0:T(8,128)}, f32[1,1]{1,0:T(1,128)}) custom-call(bf16[384,640]{1,0:T(8,128)(2,1)} %get-tuple-element.12.out_in, bf16[1728,384]{1,0:T(8,128)(2,1)} %get-tuple-element.13.fisher_in, f32[80,1728]{1,0:T(8,128)} %get-tuple-element.14.grad_in, ...), custom_call_target="tpu_custom_call" | custom-call | tf_op jit(solution)/shard_map/pallas_call | solution.py:563
